TPU v7x, 32 devices: a whole 2x2x4 slice. The times are simulated.
32 devices in a mesh: space: 16 (over z, y, x), mem: 2 (over core).
Axes of the slice: x: 2, y: 2, z: 4, core: 2. Of those that a mesh axis runs over, the one named last changes fastest.
Arguments:
- perturb: float32 [1024, 4096], P(('space', 'mem')), may hold values from -6 to 6
- pair_list: int32 [64, 3], P('space'), may hold values from 0 to 15, as said below
- pair_count: int32 [16], P('space'), may hold values from 1 to 4, as said below
- band_weight: float32 [8], replicated, may hold values from 0.25 to 1
- cov_scale: float32 [1], replicated, may hold values from 0.5 to 2
- target: float32 [4096, 1024], P('space', 'mem'), may hold values from -6 to 6
- first_guess: float32 [4096, 1024], P('space', 'mem'), may hold values from -6 to 6
Outputs:
- solution: float32 [4096, 1024], P('space', 'mem')
Inputs may be any that keep to these rules, and one draw needn't show every extreme that they name: `pair_list`: rows 4 * s to 4 * s + 3 are owner s's slots. The first block of each is owner s's own block s; the second is the first plus d modulo 16, with 0 <= d <= 3; each of the four pairs (d = 0 to 3) stands in exactly one slot of its owner. The third column is an index into band_weight. Only the first pair_count[s] slots of owner s are live; in every draw some owner has all 4 slots live.
All inputs are finite; a program needn't handle non-finite values.
Results may differ from a plain program's by a relative error of at most 0.0003.
Values sent between devices are 32-bit elements; how exact they have to be, the bound alone decides.
A program may use at most 64 MiB of HBM per device.

v0:
```python
import jax
import jax.numpy as jnp
from jax import lax
from jax.sharding import PartitionSpec as P

BLOCK = 256
MEMBERS = 1024
REACH_DEV = 3
NBANDS = 8
ITERS = 2


def shifted(array, axis, by):
    count = lax.axis_size(axis)
    return lax.ppermute(array, axis, [(i, (i + by) % count) for i in range(count)])


def fetch_members(own_members):
    pieces = [own_members]
    for offset in range(1, REACH_DEV + 1):
        pieces.append(shifted(own_members, "space", -offset))
    return jnp.concatenate(pieces, axis=1)


def fetch_field(iterate):
    pieces = [iterate]
    for offset in range(1, REACH_DEV + 1):
        pieces.append(shifted(iterate, "space", -offset))
    return jnp.concatenate(pieces, axis=0)


def return_partials(pieces):
    total = pieces[0]
    for offset in range(1, REACH_DEV + 1):
        total = total + shifted(pieces[offset], "space", offset)
    return total


def per_device(perturb, pair_list, pair_count, band_weight, cov_scale, target, first_guess):
    own_members = lax.all_to_all(perturb, "space", split_axis=1, concat_axis=0, tiled=True)
    rows_dev = own_members.shape[1]
    blocks_dev = rows_dev // BLOCK
    blocks_near = (REACH_DEV + 1) * blocks_dev
    blocks_all = blocks_dev * lax.axis_size("space")
    slot_total = pair_list.shape[0]
    first_local = (pair_list[:, 0] - lax.axis_index("space") * blocks_dev) % blocks_all
    second_local = (pair_list[:, 1] - lax.axis_index("space") * blocks_dev) % blocks_all
    living = (jnp.arange(slot_total, dtype=jnp.int32) < pair_count[0]).astype(jnp.float32)
    band_table = (pair_list[:, 2][:, None] == jnp.arange(NBANDS, dtype=jnp.int32)[None, :]).astype(
        jnp.float32
    )
    band_now = jnp.dot(
        band_table, band_weight, precision=lax.Precision.HIGHEST, preferred_element_type=jnp.float32
    )
    weights = cov_scale[0] * band_now * living / (MEMBERS - 1)
    members_near = fetch_members(own_members)

    def build_tile(slot_pair):
        first_cols = lax.dynamic_slice_in_dim(members_near, slot_pair[0] * BLOCK, BLOCK, 1)
        second_cols = lax.dynamic_slice_in_dim(members_near, slot_pair[1] * BLOCK, BLOCK, 1)
        return jnp.einsum(
            "ma,mb->ab",
            first_cols,
            second_cols,
            precision=lax.Precision.HIGHEST,
            preferred_element_type=jnp.float32,
        )

    partial_value = (
        lax.map(build_tile, jnp.stack([first_local, second_local], 1)) * weights[:, None, None]
    )
    tiles = lax.psum(partial_value, "mem")
    block_ids = jnp.arange(blocks_near, dtype=jnp.int32)
    first_select = (first_local[:, None] == block_ids[None, :]).astype(jnp.float32)
    second_select = (second_local[:, None] == block_ids[None, :]).astype(jnp.float32)
    mirror_mask = (first_local != second_local).astype(jnp.float32)
    iterate = first_guess
    columns = iterate.shape[1]
    for sweep in range(ITERS):
        field_near = fetch_field(iterate).reshape(blocks_near, BLOCK, columns)
        near_blocks = jnp.take(field_near, second_local, axis=0)
        own_blocks = jnp.take(field_near, first_local, axis=0)
        forward = jnp.einsum(
            "pab,pbc->pac",
            tiles,
            near_blocks,
            precision=lax.Precision.HIGHEST,
            preferred_element_type=jnp.float32,
        )
        mirror = jnp.einsum(
            "pab,pac->pbc",
            tiles,
            own_blocks,
            precision=lax.Precision.HIGHEST,
            preferred_element_type=jnp.float32,
        )
        mirror = mirror * mirror_mask[:, None, None]
        collected = jnp.einsum(
            "pl,pac->lac",
            first_select,
            forward,
            precision=lax.Precision.HIGHEST,
            preferred_element_type=jnp.float32,
        )
        collected = collected + jnp.einsum(
            "pl,pac->lac",
            second_select,
            mirror,
            precision=lax.Precision.HIGHEST,
            preferred_element_type=jnp.float32,
        )
        applied = return_partials([collected[offset] for offset in range(REACH_DEV + 1)])
        iterate = iterate + 0.5 * (target - iterate - applied)
    return iterate


def solution(mesh):
    in_specs = (
        P(("space", "mem"), None),
        P("space", None),
        P("space"),
        P(),
        P(),
        P("space", "mem"),
        P("space", "mem"),
    )
    out_specs = P("space", "mem")
    return jax.shard_map(
        per_device, mesh=mesh, in_specs=in_specs, out_specs=out_specs, check_vma=False
    )
```

profile of v0, /device:TPU:2, one launch (start us, length us, event | category | flops | bytes accessed | tf_op | source)
XLA Modules:
  0.0 288.0 jit_solution(15387314568821327748)
XLA Ops:
  6.5 1.9 copy.56
  8.5 7.3 %all-to-all-start = ((f32[32,16,256]{2,0,1:T(8,128)}), f32[32,16,256]{2,0,1:T(8,128)S(1)}, u32[]{:S(2)}, u32[]{:S(2)}) async-start(f32[32,16,256]{2,0,1:T(8,128)} %bitcast.87), calls=%async_computation | async-start | bytes 1048576 | tf_op jit(solution)/shard_map/all_to_all | solution.py:40
  15.9 4.2 %collective-permute-start.4 = (f32[256,512]{1,0:T(8,128)S(1)}, f32[256,512]{1,0:T(8,128)}, u32[]{:S(2)}, u32[]{:S(2)}) collective-permute-start(f32[256,512]{1,0:T(8,128)S(1)} %copy-done.8), channel_id=1, source_target_pairs={{0,28},{2,30},{4,0},{6,2},{8,4},{10,6},{12,8},{14,10},{16,12},{18,... | collective-permute-start | bytes 1572872 | tf_op jit(solution)/shard_map/ppermute | solution.py:15
  20.1 0.6 collective-permute-start.3
  21.9 0.2 slice_reduce_fusion
  22.1 0.1 copy.21
  22.2 0.1 copy.22
  22.4 7.6 %all-to-all-done = f32[32,16,256]{2,0,1:T(8,128)S(1)} async-done(((f32[32,16,256]{2,0,1:T(8,128)}), f32[32,16,256]{2,0,1:T(8,128)S(1)}, u32[]{:S(2)}, u32[]{:S(2)}) %all-to-all-start) | async-done | bytes 524320 | tf_op jit(solution)/shard_map/all_to_all | solution.py:40
  29.9 23.3 %collective-permute-start.2 = (f32[512,256]{1,0:T(8,128)S(1)}, f32[512,256]{1,0:T(8,128)S(1)}, u32[]{:S(2)}, u32[]{:S(2)}) collective-permute-start(f32[512,256]{1,0:T(8,128)S(1)} %bitcast.103), channel_id=1, source_target_pairs={{0,26},{2,28},{4,30},{6,0},{8,2},{10,4},{12,6},{14,8},{16,10},{18,... | collective-permute-start | bytes 1572872 | tf_op jit(solution)/shard_map/ppermute | solution.py:15
  53.3 1.8 collective-permute-start.1
  55.0 1.3 collective-permute-start
  56.3 0.2 fusion.23
  56.6 9.0 %collective-permute-done.2 = f32[512,256]{1,0:T(8,128)S(1)} collective-permute-done((f32[512,256]{1,0:T(8,128)S(1)}, f32[512,256]{1,0:T(8,128)S(1)}, u32[]{:S(2)}, u32[]{:S(2)}) %collective-permute-start.2) | collective-permute-done | bytes 524320 | tf_op jit(solution)/shard_map/ppermute | solution.py:15
  65.6 6.2 %collective-permute-start.5 = (f32[256,512]{1,0:T(8,128)S(1)}, f32[256,512]{1,0:T(8,128)}, u32[]{:S(2)}, u32[]{:S(2)}) collective-permute-start(f32[256,512]{1,0:T(8,128)S(1)} %copy-done.8), channel_id=1, source_target_pairs={{0,26},{2,28},{4,30},{6,0},{8,2},{10,4},{12,6},{14,8},{16,10},{18,... | collective-permute-start | bytes 1572872 | tf_op jit(solution)/shard_map/ppermute | solution.py:15
  71.8 4.9 %collective-permute-done.1 = f32[512,256]{1,0:T(8,128)S(1)} collective-permute-done((f32[512,256]{1,0:T(8,128)S(1)}, f32[512,256]{1,0:T(8,128)S(1)}, u32[]{:S(2)}, u32[]{:S(2)}) %collective-permute-start.1) | collective-permute-done | bytes 524320 | tf_op jit(solution)/shard_map/ppermute | solution.py:15
  76.7 3.1 %collective-permute-done = f32[512,256]{1,0:T(8,128)S(1)} collective-permute-done((f32[512,256]{1,0:T(8,128)S(1)}, f32[512,256]{1,0:T(8,128)S(1)}, u32[]{:S(2)}, u32[]{:S(2)}) %collective-permute-start) | collective-permute-done | bytes 524320 | tf_op jit(solution)/shard_map/ppermute | solution.py:15
  79.9 0.3 pad_maximum_fusion
  80.1 15.1 %while.10 = (s32[]{:T(128)}, f32[4,256,256]{2,1,0:T(8,128)}, s32[4,2]{0,1:T(2,128)S(1)}, f32[512,1024]{1,0:T(8,128)S(1)}, s32[]{:T(128)}, /*index=5*/s32[1,1]{0,1:T(1,128)}, s32[]{:T(128)}, s32[]{:T(128)}) while((s32[]{:T(128)}, f32[4,256,256]{2,1,0:T(8,128)}, s32[4,2]{0,1:T(2,128)S(1)}, f32[512,1024]{1,0:T(8,128)S(1)}, s32[]{:T(128)}, ...), condition=%wide.region_1.2_spmd, body=%wide.region_0.1_spmd.sunk | while | flops 402653184 | bytes 1310953 | solution.py:70
  80.1 0.1 constant_dynamic-slice_fusion.2
  80.2 0.6 fusion.78
  82.2 1.7 fusion.79
  84.0 0.6 fusion.78
  85.9 1.8 fusion.79
  87.7 0.6 fusion.78
  89.7 1.8 fusion.79
  91.5 0.6 fusion.78
  93.5 1.8 fusion.79
  95.2 2.4 broadcast_multiply_fusion
  97.7 3.7 %collective-permute-done.5 = f32[256,512]{1,0:T(8,128)} collective-permute-done((f32[256,512]{1,0:T(8,128)S(1)}, f32[256,512]{1,0:T(8,128)}, u32[]{:S(2)}, u32[]{:S(2)}) %collective-permute-start.5) | collective-permute-done | bytes 524320 | tf_op jit(solution)/shard_map/ppermute | solution.py:15
  101.4 1.6 pad_maximum_fusion.1
  103.0 2.0 gather_fusion.1
  105.0 2.0 gather_fusion
  107.1 26.6 %all-reduce.2.cloned.1.call-done = f32[4,256,256]{2,1,0:T(8,128)} async-done(((f32[4,256,256]{2,1,0:T(8,128)}), f32[4,256,256]{2,1,0:T(8,128)}) %all-reduce.2.cloned.1.call-update) | async-done | bytes 1048592 | tf_op jit(solution)/shard_map/psum | solution.py:72
  133.7 4.2 %fusion.14 = f32[4,256,512]{2,1,0:T(8,128)S(1)} fusion(f32[4,256,256]{2,1,0:T(8,128)} %all-reduce.2.cloned.1.call-done, f32[4,256,512]{2,1,0:T(8,128)} %gather_fusion.1, pred[4]{0:T(512)(128)(4,1)S(1)} %compare_and_fusion), kind=kOutput, calls=%fused_computation.26 | convolution fusion | flops 1611137024 | bytes 5242884 | tf_op jit(solution)/shard_map/pab,pac->pbc/dot_general | solution.py:90
  137.9 3.3 %fusion.7 = f32[4,256,512]{2,0,1:T(4,128)S(1)} fusion(f32[4,256,512]{2,1,0:T(8,128)S(1)} %fusion.14, f32[4]{0:T(128)S(1)} %get-tuple-element.39, s32[4]{0:T(128)S(1)} %bitcast.113), kind=kOutput, calls=%fused_computation.18 | convolution fusion | flops 25690128 | bytes 4194336 | tf_op jit(solution)/shard_map/pl,pac->lac/dot_general | solution.py:105
  141.3 2.1 fusion.16
  143.4 3.8 %fusion.18 = f32[4,256,512]{2,0,1:T(4,128)S(1)} fusion(f32[4,256,512]{2,0,1:T(4,128)S(1)} %fusion.7, f32[4,256,512]{2,1,0:T(8,128)S(1)} %fusion.16, s32[4]{0:T(128)S(1)} %bitcast.111), kind=kOutput, calls=%fused_computation.30 | convolution fusion | flops 25690128 | bytes 6291472 | tf_op jit(solution)/shard_map/pl,pac->lac/dot_general | solution.py:98
  147.2 1.5 fusion.67
  148.9 1.5 collective-permute-start.7
  150.4 1.5 collective-permute-start.8
  151.9 2.4 collective-permute-start.6
  154.2 19.0 %collective-permute-done.7 = f32[256,512]{1,0:T(8,128)S(1)} collective-permute-done((f32[256,512]{1,0:T(8,128)S(1)}, f32[256,512]{1,0:T(8,128)S(1)}, u32[]{:S(2)}, u32[]{:S(2)}) %collective-permute-start.7) | collective-permute-done | bytes 524320 | tf_op jit(solution)/shard_map/ppermute | solution.py:15
  173.3 3.7 %collective-permute-done.8 = f32[256,512]{1,0:T(8,128)S(1)} collective-permute-done((f32[256,512]{1,0:T(8,128)S(1)}, f32[256,512]{1,0:T(8,128)S(1)}, u32[]{:S(2)}, u32[]{:S(2)}) %collective-permute-start.8) | collective-permute-done | bytes 524320 | tf_op jit(solution)/shard_map/ppermute | solution.py:15
  177.0 0.4 fusion.45
  177.3 3.7 %collective-permute-start.11 = (f32[256,512]{1,0:T(8,128)S(1)}, f32[256,512]{1,0:T(8,128)S(1)}, u32[]{:S(2)}, u32[]{:S(2)}) collective-permute-start(f32[256,512]{1,0:T(8,128)S(1)} %fusion.45), channel_id=1, source_target_pairs={{0,26},{2,28},{4,30},{6,0},{8,2},{10,4},{12,6},{14,8},{16,10},{18,... | collective-permute-start | bytes 1572872 | tf_op jit(solution)/shard_map/ppermute | solution.py:15
  181.0 11.5 %collective-permute-start.10 = (f32[256,512]{1,0:T(8,128)S(1)}, f32[256,512]{1,0:T(8,128)S(1)}, u32[]{:S(2)}, u32[]{:S(2)}) collective-permute-start(f32[256,512]{1,0:T(8,128)S(1)} %fusion.45), channel_id=1, source_target_pairs={{0,28},{2,30},{4,0},{6,2},{8,4},{10,6},{12,8},{14,10},{16,12},{18,... | collective-permute-start | bytes 1572872 | tf_op jit(solution)/shard_map/ppermute | solution.py:15
  192.5 9.5 %collective-permute-done.11 = f32[256,512]{1,0:T(8,128)S(1)} collective-permute-done((f32[256,512]{1,0:T(8,128)S(1)}, f32[256,512]{1,0:T(8,128)S(1)}, u32[]{:S(2)}, u32[]{:S(2)}) %collective-permute-start.11) | collective-permute-done | bytes 524320 | tf_op jit(solution)/shard_map/ppermute | solution.py:15
  202.0 12.0 %collective-permute-done.10 = f32[256,512]{1,0:T(8,128)S(1)} collective-permute-done((f32[256,512]{1,0:T(8,128)S(1)}, f32[256,512]{1,0:T(8,128)S(1)}, u32[]{:S(2)}, u32[]{:S(2)}) %collective-permute-start.10) | collective-permute-done | bytes 524320 | tf_op jit(solution)/shard_map/ppermute | solution.py:15
  214.0 0.2 pad_maximum_fusion.2
  214.2 2.0 gather_fusion.3
  216.2 2.0 gather_fusion.2
  218.2 4.0 %fusion.10 = f32[4,256,512]{2,1,0:T(8,128)S(1)} fusion(f32[4,256,256]{2,1,0:T(8,128)S(1)} %copy-done.1, f32[4,256,512]{2,1,0:T(8,128)} %gather_fusion.3, pred[4]{0:T(512)(128)(4,1)S(1)} %compare_and_fusion), kind=kOutput, calls=%fused_computation.22 | convolution fusion | flops 1611137024 | bytes 5242884 | tf_op jit(solution)/shard_map/pab,pac->pbc/dot_general | solution.py:90
  222.2 3.3 %fusion.4 = f32[4,256,512]{2,0,1:T(4,128)S(1)} fusion(f32[4,256,512]{2,1,0:T(8,128)S(1)} %fusion.10, f32[4]{0:T(128)S(1)} %get-tuple-element.39, s32[4]{0:T(128)S(1)} %bitcast.114), kind=kOutput, calls=%fused_computation.14 | convolution fusion | flops 25690128 | bytes 4194336 | tf_op jit(solution)/shard_map/pl,pac->lac/dot_general | solution.py:105
  225.6 2.1 fusion.12
  227.7 3.2 %fusion.5 = f32[4,256,512]{2,0,1:T(4,128)S(1)} fusion(f32[4,256,512]{2,1,0:T(8,128)S(1)} %fusion.12, s32[4]{0:T(128)S(1)} %bitcast.112), kind=kOutput, calls=%fused_computation.15 | convolution fusion | flops 25165840 | bytes 4194320 | tf_op jit(solution)/shard_map/pl,pac->lac/dot_general | solution.py:98
  231.0 1.2 copy_add_fusion
  232.2 0.1 slice_bitcast_fusion.2
  232.3 1.6 collective-permute-start.12
  233.9 7.3 %collective-permute-start.14 = (f32[256,512]{1,0:T(8,128)S(1)}, f32[256,512]{1,0:T(8,128)S(1)}, u32[]{:S(2)}, u32[]{:S(2)}) collective-permute-start(f32[256,512]{1,0:T(8,128)S(1)} %get-tuple-element.44), channel_id=1, source_target_pairs={{0,6},{2,8},{4,10},{6,12},{8,14},{10,16},{12,18},{14,20},{16,22},{... | collective-permute-start | bytes 1572872 | tf_op jit(solution)/shard_map/ppermute | solution.py:15
  241.2 4.8 %collective-permute-start.13 = (f32[256,512]{1,0:T(8,128)S(1)}, f32[256,512]{1,0:T(8,128)S(1)}, u32[]{:S(2)}, u32[]{:S(2)}) collective-permute-start(f32[256,512]{1,0:T(8,128)S(1)} %get-tuple-element.45), channel_id=1, source_target_pairs={{0,4},{2,6},{4,8},{6,10},{8,12},{10,14},{12,16},{14,18},{16,20},{1... | collective-permute-start | bytes 1572872 | tf_op jit(solution)/shard_map/ppermute | solution.py:15
  246.0 8.8 %collective-permute-done.12 = f32[256,512]{1,0:T(8,128)S(1)} collective-permute-done((f32[256,512]{1,0:T(8,128)S(1)}, f32[256,512]{1,0:T(8,128)S(1)}, u32[]{:S(2)}, u32[]{:S(2)}) %collective-permute-start.12) | collective-permute-done | bytes 524320 | tf_op jit(solution)/shard_map/ppermute | solution.py:15
  254.8 6.1 %collective-permute-done.14 = f32[256,512]{1,0:T(8,128)S(1)} collective-permute-done((f32[256,512]{1,0:T(8,128)S(1)}, f32[256,512]{1,0:T(8,128)S(1)}, u32[]{:S(2)}, u32[]{:S(2)}) %collective-permute-start.14) | collective-permute-done | bytes 524320 | tf_op jit(solution)/shard_map/ppermute | solution.py:15
  260.9 19.1 %collective-permute-done.13 = f32[256,512]{1,0:T(8,128)S(1)} collective-permute-done((f32[256,512]{1,0:T(8,128)S(1)}, f32[256,512]{1,0:T(8,128)S(1)}, u32[]{:S(2)}, u32[]{:S(2)}) %collective-permute-start.13) | collective-permute-done | bytes 524320 | tf_op jit(solution)/shard_map/ppermute | solution.py:15
  280.0 1.2 fusion.39
  (43 shorter events, 0.5 us)
Async XLA Ops:
  6.5 49.8 %copy-start = (f32[8]{0:T(128)S(1)}, f32[8]{0:T(128)}, u32[]{:S(2)}) copy-start(f32[8]{0:T(128)} %param.14) | copy-start | bytes 100
  6.5 9.3 %copy-start.8 = (f32[256,512]{1,0:T(8,128)S(1)}, f32[256,512]{1,0:T(8,128)}, u32[]{:S(2)}) copy-start(f32[256,512]{1,0:T(8,128)} %param.17) | copy-start | bytes 1572868
  6.5 15.4 %copy-start.9 = (s32[4,3]{1,0:T(4,128)S(1)}, s32[4,3]{1,0:T(4,128)}, u32[]{:S(2)}) copy-start(s32[4,3]{1,0:T(4,128)} %param.12) | copy-start | bytes 148
  8.5 21.4 %all-to-all-start = ((f32[32,16,256]{2,0,1:T(8,128)}), f32[32,16,256]{2,0,1:T(8,128)S(1)}, u32[]{:S(2)}, u32[]{:S(2)}) async-start(f32[32,16,256]{2,0,1:T(8,128)} %bitcast.87), calls=%async_computation | async-start | bytes 1048576 | tf_op jit(solution)/shard_map/all_to_all | solution.py:40
  15.8 117.9 %all-reduce.2.cloned.1.call-start = ((), (), s32[]{:S(2)}) async-start(), calls=%async_computation.1 | async-start | bytes 2097152 | tf_op jit(solution)/shard_map/psum | solution.py:72
  15.9 81.9 %collective-permute-start.4 = (f32[256,512]{1,0:T(8,128)S(1)}, f32[256,512]{1,0:T(8,128)}, u32[]{:S(2)}, u32[]{:S(2)}) collective-permute-start(f32[256,512]{1,0:T(8,128)S(1)} %copy-done.8), channel_id=1, source_target_pairs={{0,28},{2,30},{4,0},{6,2},{8,4},{10,6},{12,8},{14,10},{16,12},{18,... | collective-permute-start | bytes 1572872 | tf_op jit(solution)/shard_map/ppermute | solution.py:15
  20.1 77.6 %collective-permute-start.3 = (f32[256,512]{1,0:T(8,128)S(1)}, f32[256,512]{1,0:T(8,128)}, u32[]{:S(2)}, u32[]{:S(2)}) collective-permute-start(f32[256,512]{1,0:T(8,128)S(1)} %copy-done.8), channel_id=1, source_target_pairs={{0,30},{2,0},{4,2},{6,4},{8,6},{10,8},{12,10},{14,12},{16,14},{18,... | collective-permute-start | bytes 1572872 | tf_op jit(solution)/shard_map/ppermute | solution.py:15
  29.9 35.7 %collective-permute-start.2 = (f32[512,256]{1,0:T(8,128)S(1)}, f32[512,256]{1,0:T(8,128)S(1)}, u32[]{:S(2)}, u32[]{:S(2)}) collective-permute-start(f32[512,256]{1,0:T(8,128)S(1)} %bitcast.103), channel_id=1, source_target_pairs={{0,26},{2,28},{4,30},{6,0},{8,2},{10,4},{12,6},{14,8},{16,10},{18,... | collective-permute-start | bytes 1572872 | tf_op jit(solution)/shard_map/ppermute | solution.py:15
  53.3 23.5 %collective-permute-start.1 = (f32[512,256]{1,0:T(8,128)S(1)}, f32[512,256]{1,0:T(8,128)S(1)}, u32[]{:S(2)}, u32[]{:S(2)}) collective-permute-start(f32[512,256]{1,0:T(8,128)S(1)} %bitcast.104), channel_id=1, source_target_pairs={{0,28},{2,30},{4,0},{6,2},{8,4},{10,6},{12,8},{14,10},{16,12},{18,... | collective-permute-start | bytes 1572872 | tf_op jit(solution)/shard_map/ppermute | solution.py:15
  55.0 24.8 %collective-permute-start = (f32[512,256]{1,0:T(8,128)S(1)}, f32[512,256]{1,0:T(8,128)S(1)}, u32[]{:S(2)}, u32[]{:S(2)}) collective-permute-start(f32[512,256]{1,0:T(8,128)S(1)} %bitcast.105), channel_id=1, source_target_pairs={{0,30},{2,0},{4,2},{6,4},{8,6},{10,8},{12,10},{14,12},{16,14},{18,... | collective-permute-start | bytes 1572872 | tf_op jit(solution)/shard_map/ppermute | solution.py:15
  65.6 35.9 %collective-permute-start.5 = (f32[256,512]{1,0:T(8,128)S(1)}, f32[256,512]{1,0:T(8,128)}, u32[]{:S(2)}, u32[]{:S(2)}) collective-permute-start(f32[256,512]{1,0:T(8,128)S(1)} %copy-done.8), channel_id=1, source_target_pairs={{0,26},{2,28},{4,30},{6,0},{8,2},{10,4},{12,6},{14,8},{16,10},{18,... | collective-permute-start | bytes 1572872 | tf_op jit(solution)/shard_map/ppermute | solution.py:15
  137.9 3.4 %copy-start.1 = (f32[4,256,256]{2,1,0:T(8,128)S(1)}, f32[4,256,256]{2,1,0:T(8,128)}, u32[]{:S(2)}) copy-start(f32[4,256,256]{2,1,0:T(8,128)} %all-reduce.2.cloned.1.call-done) | copy-start | bytes 3145732
  137.9 3.4 %copy-start.2 = (f32[4,256,512]{2,1,0:T(8,128)S(1)}, f32[4,256,512]{2,1,0:T(8,128)}, u32[]{:S(2)}) copy-start(f32[4,256,512]{2,1,0:T(8,128)} %gather_fusion) | copy-start | bytes 6291460
  148.7 28.2 %copy-start.6 = (f32[256,512]{1,0:T(8,128)S(1)}, f32[256,512]{1,0:T(8,128)}, u32[]{:S(2)}) copy-start(f32[256,512]{1,0:T(8,128)} %param.16) | copy-start | bytes 1572868
  148.9 24.4 %collective-permute-start.7 = (f32[256,512]{1,0:T(8,128)S(1)}, f32[256,512]{1,0:T(8,128)S(1)}, u32[]{:S(2)}, u32[]{:S(2)}) collective-permute-start(f32[256,512]{1,0:T(8,128)S(1)} %bitcast.110), channel_id=1, source_target_pairs={{0,4},{2,6},{4,8},{6,10},{8,12},{10,14},{12,16},{14,18},{16,20},{1... | collective-permute-start | bytes 1572872 | tf_op jit(solution)/shard_map/ppermute | solution.py:15
  150.4 26.6 %collective-permute-start.8 = (f32[256,512]{1,0:T(8,128)S(1)}, f32[256,512]{1,0:T(8,128)S(1)}, u32[]{:S(2)}, u32[]{:S(2)}) collective-permute-start(f32[256,512]{1,0:T(8,128)S(1)} %bitcast.109), channel_id=1, source_target_pairs={{0,6},{2,8},{4,10},{6,12},{8,14},{10,16},{12,18},{14,20},{16,22},{... | collective-permute-start | bytes 1572872 | tf_op jit(solution)/shard_map/ppermute | solution.py:15
  151.9 25.1 %collective-permute-start.6 = (f32[256,512]{1,0:T(8,128)S(1)}, f32[256,512]{1,0:T(8,128)S(1)}, u32[]{:S(2)}, u32[]{:S(2)}) collective-permute-start(f32[256,512]{1,0:T(8,128)S(1)} %bitcast.108), channel_id=1, source_target_pairs={{0,2},{2,4},{4,6},{6,8},{8,10},{10,12},{12,14},{14,16},{16,18},{18... | collective-permute-start | bytes 1572872 | tf_op jit(solution)/shard_map/ppermute | solution.py:15
  177.3 36.9 %copy-start.4 = (f32[256,512]{1,0:T(8,128)}, f32[256,512]{1,0:T(8,128)S(1)}, u32[]{:S(2)}) copy-start(f32[256,512]{1,0:T(8,128)S(1)} %fusion.45) | copy-start | bytes 1572868
  177.3 24.7 %collective-permute-start.11 = (f32[256,512]{1,0:T(8,128)S(1)}, f32[256,512]{1,0:T(8,128)S(1)}, u32[]{:S(2)}, u32[]{:S(2)}) collective-permute-start(f32[256,512]{1,0:T(8,128)S(1)} %fusion.45), channel_id=1, source_target_pairs={{0,26},{2,28},{4,30},{6,0},{8,2},{10,4},{12,6},{14,8},{16,10},{18,... | collective-permute-start | bytes 1572872 | tf_op jit(solution)/shard_map/ppermute | solution.py:15
  181.0 33.0 %collective-permute-start.10 = (f32[256,512]{1,0:T(8,128)S(1)}, f32[256,512]{1,0:T(8,128)S(1)}, u32[]{:S(2)}, u32[]{:S(2)}) collective-permute-start(f32[256,512]{1,0:T(8,128)S(1)} %fusion.45), channel_id=1, source_target_pairs={{0,28},{2,30},{4,0},{6,2},{8,4},{10,6},{12,8},{14,10},{16,12},{18,... | collective-permute-start | bytes 1572872 | tf_op jit(solution)/shard_map/ppermute | solution.py:15
  192.5 21.5 %collective-permute-start.9 = (f32[256,512]{1,0:T(8,128)S(1)}, f32[256,512]{1,0:T(8,128)S(1)}, u32[]{:S(2)}, u32[]{:S(2)}) collective-permute-start(f32[256,512]{1,0:T(8,128)S(1)} %fusion.45), channel_id=1, source_target_pairs={{0,30},{2,0},{4,2},{6,4},{8,6},{10,8},{12,10},{14,12},{16,14},{18,... | collective-permute-start | bytes 1572872 | tf_op jit(solution)/shard_map/ppermute | solution.py:15
  222.2 3.4 %copy-start.3 = (f32[4,256,512]{2,1,0:T(8,128)S(1)}, f32[4,256,512]{2,1,0:T(8,128)}, u32[]{:S(2)}) copy-start(f32[4,256,512]{2,1,0:T(8,128)} %gather_fusion.2) | copy-start | bytes 6291460
  232.2 47.8 %copy-start.5 = (f32[256,512]{1,0:T(8,128)S(1)}, f32[256,512]{1,0:T(8,128)}, u32[]{:S(2)}) copy-start(f32[256,512]{1,0:T(8,128)} %copy-done.4) | copy-start | bytes 1572868
  232.2 47.8 %copy-start.7 = (f32[256,512]{1,0:T(8,128)S(1)}, f32[256,512]{1,0:T(8,128)}, u32[]{:S(2)}) copy-start(f32[256,512]{1,0:T(8,128)} %param.16) | copy-start | bytes 1572868
  232.3 22.4 %collective-permute-start.12 = (f32[256,512]{1,0:T(8,128)S(1)}, f32[256,512]{1,0:T(8,128)S(1)}, u32[]{:S(2)}, u32[]{:S(2)}) collective-permute-start(f32[256,512]{1,0:T(8,128)S(1)} %get-tuple-element.43), channel_id=1, source_target_pairs={{0,2},{2,4},{4,6},{6,8},{8,10},{10,12},{12,14},{14,16},{16,18},{18... | collective-permute-start | bytes 1572872 | tf_op jit(solution)/shard_map/ppermute | solution.py:15
  233.9 27.0 %collective-permute-start.14 = (f32[256,512]{1,0:T(8,128)S(1)}, f32[256,512]{1,0:T(8,128)S(1)}, u32[]{:S(2)}, u32[]{:S(2)}) collective-permute-start(f32[256,512]{1,0:T(8,128)S(1)} %get-tuple-element.44), channel_id=1, source_target_pairs={{0,6},{2,8},{4,10},{6,12},{8,14},{10,16},{12,18},{14,20},{16,22},{... | collective-permute-start | bytes 1572872 | tf_op jit(solution)/shard_map/ppermute | solution.py:15
  241.2 38.8 %collective-permute-start.13 = (f32[256,512]{1,0:T(8,128)S(1)}, f32[256,512]{1,0:T(8,128)S(1)}, u32[]{:S(2)}, u32[]{:S(2)}) collective-permute-start(f32[256,512]{1,0:T(8,128)S(1)} %get-tuple-element.45), channel_id=1, source_target_pairs={{0,4},{2,6},{4,8},{6,10},{8,12},{10,14},{12,16},{14,18},{16,20},{1... | collective-permute-start | bytes 1572872 | tf_op jit(solution)/shard_map/ppermute | solution.py:15
Sparse Core Ops, SparseCore 0:
  97.8 35.9 all-reduce.1
where the time goes:
time: 288 us
  waiting for transfers between devices  133 us (46%)
  starting transfers between devices  79 us (27%)
  matrix products  33.3 us (12%)
  between operations  15 us (5%)
  local copies, waits for them, and re-layouts  14.9 us (5%)
  other arithmetic  7.2 us (2%)
  loops' own time  5.42 us (2%)
    ppermute x15, waiting for transfers between devices, shifted(): lax.ppermute(array, axis, [(i, (i + by) % count) for i in range(count)])  99 us
    ppermute x15, starting transfers between devices, shifted(): lax.ppermute(array, axis, [(i, (i + by) % count) for i in range(count)])  71.7 us
    psum x1, waiting for transfers between devices, per_device(): tiles = lax.psum(partial_value, 'mem')  26.6 us
    dot_general x2, matrix products, per_device(): jnp.einsum('pab,pac->pbc', tiles, own_blocks, precision=lax.Precision.HIG...  8.13 us
    all_to_all x1, waiting for transfers between devices, per_device(): lax.all_to_all(perturb, 'space', split_axis=1, concat_axis=0, tiled=True)  7.55 us
    all_to_all x1, starting transfers between devices, per_device(): lax.all_to_all(perturb, 'space', split_axis=1, concat_axis=0, tiled=True)  7.31 us
    dot_general x2, matrix products, per_device(): jnp.einsum('pl,pac->lac', first_select, forward, precision=lax.Precision....  7.02 us
    dot_general x4, matrix products, build_tile(): jnp.einsum('ma,mb->ab', first_cols, second_cols, precision=lax.Precision....  7.01 us
  transfers between devices with their start and end apart: 17, of which 13 were waited for; matrix products, arithmetic and copies ran while one was open for 6% of the time, Pallas kernels for 0%

commit v1 on v0

v1 whole, which is shorter than its diff:
```python
import jax
import jax.numpy as jnp
from jax import lax
from jax.sharding import PartitionSpec as P

BLOCK = 256
MEMBERS = 1024
REACH_DEV = 3
NBANDS = 8
ITERS = 2


def shifted(array, axis, by):
    count = lax.axis_size(axis)
    return lax.ppermute(array, axis, [(i, (i + by) % count) for i in range(count)])


def mm(a, b, ca, cb):
    return lax.dot_general(
        a, b, (((ca,), (cb,)), ((), ())), precision=lax.Precision.HIGH,
        preferred_element_type=jnp.float32,
    )


def gap_weights(pair_list, pair_count, band_weight, cov_scale):
    slots = pair_list.shape[0]
    blocks_all = lax.axis_size("space")
    gap = (pair_list[:, 1] - pair_list[:, 0]) % blocks_all
    living = (jnp.arange(slots, dtype=jnp.int32) < pair_count[0]).astype(jnp.float32)
    bands = jnp.arange(NBANDS, dtype=jnp.int32)
    band_now = jnp.sum(
        jnp.where(pair_list[:, 2][:, None] == bands[None, :], band_weight[None, :], 0.0), axis=1
    )
    slot_weight = cov_scale[0] * band_now * living / (MEMBERS - 1)
    gaps = jnp.arange(REACH_DEV + 1, dtype=jnp.int32)
    return jnp.sum(jnp.where(gap[:, None] == gaps[None, :], slot_weight[:, None], 0.0), axis=0)


def per_device(perturb, pair_list, pair_count, band_weight, cov_scale, target, first_guess):
    w = gap_weights(pair_list, pair_count, band_weight, cov_scale)
    w_next = shifted(w, "space", -1)
    p0 = lax.all_to_all(perturb, "space", split_axis=1, concat_axis=0, tiled=True)
    p1 = shifted(p0, "space", -1)
    p3 = shifted(p0, "space", -3)
    x0 = first_guess
    t0 = mm(p0, p0, 0, 0) * w[0]
    t1 = mm(p0, p1, 0, 0) * w[1]
    t3 = mm(p0, p3, 0, 0) * w[3]
    t2 = mm(p1, p3, 0, 0) * w_next[2]
    t0, t1, t2, t3 = lax.psum((t0, t1, t2, t3), "mem")
    for sweep in range(ITERS):
        x1 = shifted(x0, "space", -1)
        x3 = shifted(x0, "space", -3)
        back1 = shifted(mm(t1, x0, 0, 0) + mm(t2, x3, 1, 0), "space", 1)
        back3 = shifted(mm(t3, x0, 0, 0) + mm(t2, x1, 0, 0), "space", 3)
        own = mm(t0, x0, 1, 0) + mm(t1, x1, 1, 0) + mm(t3, x3, 1, 0)
        x0 = x0 + 0.5 * (target - x0 - (own + back1 + back3))
    return x0


def solution(mesh):
    in_specs = (
        P(("space", "mem"), None),
        P("space", None),
        P("space"),
        P(),
        P(),
        P("space", "mem"),
        P("space", "mem"),
    )
    out_specs = P("space", "mem")
    return jax.shard_map(
        per_device, mesh=mesh, in_specs=in_specs, out_specs=out_specs, check_vma=False
    )
```

time: 288 us -> 172 us (0.60)
  the two profiles are of different devices: /device:TPU:2 before, /device:TPU:28 now
where the time goes in v1:
time: 172 us; the launch traced here: 170 us
  waiting for transfers between devices  111 us (65%)
  starting transfers between devices  22.5 us (13%)
  matrix products  15.3 us (9%)
  between operations  14.9 us (9%)
  local copies, waits for them, and re-layouts  5.37 us (3%)
    ppermute x11, waiting for transfers between devices, shifted(): lax.ppermute(array, axis, [(i, (i + by) % count) for i in range(count)])  83.4 us
    psum x1, waiting for transfers between devices, per_device(): t0, t1, t2, t3 = lax.psum((t0, t1, t2, t3), 'mem')  17.2 us
    ppermute x11, starting transfers between devices, shifted(): lax.ppermute(array, axis, [(i, (i + by) % count) for i in range(count)])  15.5 us
    dot_general x18, matrix products, mm(): lax.dot_general(a, b, (((ca,), (cb,)), ((), ())), precision=lax.Precision...  15.3 us
    all_to_all x1, waiting for transfers between devices, per_device(): lax.all_to_all(perturb, 'space', split_axis=1, concat_axis=0, tiled=True)  10.6 us
    all_to_all x1, starting transfers between devices, per_device(): lax.all_to_all(perturb, 'space', split_axis=1, concat_axis=0, tiled=True)  6.94 us
  transfers between devices with their start and end apart: 13, of which 8 were waited for; matrix products, arithmetic and copies ran while one was open for 7% of the time, Pallas kernels for 0%

profile of v1, /device:TPU:28, one launch (start us, length us, event | category | flops | bytes accessed | tf_op | source)
XLA Modules:
  0.0 169.8 jit_solution(16885605686824143802)
XLA Ops:
  6.5 1.9 %copy.12 = f32[4,16,8,256]{3,2,0,1:T(8,128)} copy(f32[4,16,8,256]{3,2,1,0:T(8,128)} %bitcast.59) | data formatting | bytes 1048576 | tf_op jit(solution)/shard_map/all_to_all | solution.py:42
  8.4 6.9 %all-to-all-start = ((f32[32,16,256]{2,0,1:T(8,128)}), f32[32,16,256]{2,0,1:T(8,128)S(1)}, u32[]{:S(2)}, u32[]{:S(2)}) async-start(f32[32,16,256]{2,0,1:T(8,128)} %bitcast.52), calls=%async_computation | async-start | bytes 1048576 | tf_op jit(solution)/shard_map/all_to_all | solution.py:42
  15.4 0.0 copy-start.6
  15.4 0.0 all-reduce.3.cloned.1.call-start
  16.7 0.0 copy-done.6
  16.7 0.2 fusion.10
  17.0 0.0 copy-start.7
  17.0 0.7 copy-done.7
  17.6 0.2 select_reduce_fusion.1
  17.8 10.6 %all-to-all-done = f32[32,16,256]{2,0,1:T(8,128)S(1)} async-done(((f32[32,16,256]{2,0,1:T(8,128)}), f32[32,16,256]{2,0,1:T(8,128)S(1)}, u32[]{:S(2)}, u32[]{:S(2)}) %all-to-all-start) | async-done | bytes 524320 | tf_op jit(solution)/shard_map/all_to_all | solution.py:42
  28.4 0.5 collective-permute-start
  28.9 0.1 select_reduce_fusion
  29.0 1.5 collective-permute-start.4
  30.5 1.5 collective-permute-start.2
  32.0 0.6 fusion.12
  32.6 17.8 %collective-permute-done.4 = f32[4]{0:T(128)S(1)} collective-permute-done((f32[4]{0:T(128)S(1)}, f32[4]{0:T(128)S(1)}, u32[]{:S(2)}, u32[]{:S(2)}) %collective-permute-start.4) | collective-permute-done | bytes 48 | tf_op jit(solution)/shard_map/ppermute | solution.py:15
  50.4 0.6 slice.27
  51.0 1.9 %fusion.7 = f32[256,256]{1,0:T(8,128)} fusion(f32[32,16,256]{2,0,1:T(8,128)S(1)} %all-to-all-done, f32[]{:T(128)} %bitcast.4), kind=kOutput, calls=%fused_computation.16 | convolution fusion | flops 201392128 | bytes 786436 | tf_op jit(solution)/shard_map/dot_general | solution.py:19
  53.0 0.0 collective-permute-done
  53.0 1.9 %convolution_multiply_fusion.2 = f32[256,256]{1,0:T(8,128)} fusion(f32[512,256]{1,0:T(8,128)S(1)} %bitcast.57, f32[512,256]{1,0:T(8,128)S(1)} %collective-permute-done, f32[]{:T(128)} %bitcast.7), kind=kOutput, calls=%fused_computation.19 | convolution fusion | flops 201392128 | bytes 1310724 | tf_op jit(solution)/shard_map/dot_general | solution.py:19
  54.8 0.0 collective-permute-done.2
  54.8 2.0 %convolution_multiply_fusion.1 = f32[256,256]{1,0:T(8,128)} fusion(f32[512,256]{1,0:T(8,128)S(1)} %bitcast.58, f32[512,256]{1,0:T(8,128)S(1)} %collective-permute-done.2, f32[]{:T(128)} %bitcast.8), kind=kOutput, calls=%fused_computation.18 | convolution fusion | flops 201392128 | bytes 1310724 | tf_op jit(solution)/shard_map/dot_general | solution.py:19
  56.8 1.9 %convolution_multiply_fusion = f32[256,256]{1,0:T(8,128)} fusion(f32[512,256]{1,0:T(8,128)S(1)} %collective-permute-done, f32[512,256]{1,0:T(8,128)S(1)} %collective-permute-done.2, f32[]{:T(128)} %bitcast.9), kind=kOutput, calls=%fused_computation.17 | convolution fusion | flops 201392128 | bytes 1310724 | tf_op jit(solution)/shard_map/dot_general | solution.py:19
  58.7 0.0 copy-start
  58.7 0.0 all-reduce.3.cloned.1.call-update
  58.7 1.0 copy-done
  59.7 0.0 collective-permute-start.3
  59.7 4.3 %collective-permute-start.1 = (f32[256,512]{1,0:T(8,128)S(1)}, f32[256,512]{1,0:T(8,128)S(1)}, u32[]{:S(2)}, u32[]{:S(2)}) collective-permute-start(f32[256,512]{1,0:T(8,128)S(1)} %copy-done), channel_id=1, source_target_pairs={{0,30},{2,0},{4,2},{6,4},{8,6},{10,8},{12,10},{14,12},{16,14},{18,... | collective-permute-start | bytes 1572872 | tf_op jit(solution)/shard_map/ppermute | solution.py:15
  64.0 17.2 %all-reduce.3.cloned.1.call-done = (f32[256,256]{1,0:T(8,128)}, f32[256,256]{1,0:T(8,128)}, f32[256,256]{1,0:T(8,128)}, f32[256,256]{1,0:T(8,128)}) async-done(((f32[256,256]{1,0:T(8,128)}, f32[256,256]{1,0:T(8,128)}, f32[256,256]{1,0:T(8,128)}, f32[256,256]{1,0:T(8,128)}), (f32[256,256]{1,0:T(8,128)}, f32[256,256]{1,0:T(8,128)}, f32[256,256]{1,0:T(8,128)}, ...) | async-done | bytes 1048592 | tf_op jit(solution)/shard_map/psum | solution.py:50
  81.3 1.4 fusion.14
  82.7 0.0 collective-permute-done.3
  82.7 0.0 copy-done.2
  82.7 0.0 copy-start.3
  82.7 0.4 convolution_add_fusion.5
  83.1 1.5 collective-permute-start.5
  84.7 0.0 copy-done.3
  84.7 0.4 fusion.15
  85.1 0.0 copy-start.5
  85.1 0.0 collective-permute-done.1
  85.1 0.4 convolution_add_fusion.4
  85.5 1.4 collective-permute-start.6
  87.0 0.0 copy-done.5
  87.0 0.4 fusion.13
  87.4 0.6 copy-done.1
  87.9 0.4 convolution_add_fusion.7
  88.3 21.1 %collective-permute-done.5 = f32[256,512]{1,0:T(8,128)S(1)} collective-permute-done((f32[256,512]{1,0:T(8,128)S(1)}, f32[256,512]{1,0:T(8,128)S(1)}, u32[]{:S(2)}, u32[]{:S(2)}) %collective-permute-start.5) | collective-permute-done | bytes 524320 | tf_op jit(solution)/shard_map/ppermute | solution.py:15
  109.4 0.0 collective-permute-done.6
  109.4 0.0 copy-done.4
  109.4 0.5 fusion.6
  109.9 2.0 %collective-permute-start.8 = (f32[256,512]{1,0:T(8,128)S(1)}, f32[256,512]{1,0:T(8,128)S(1)}, u32[]{:S(2)}, u32[]{:S(2)}) collective-permute-start(f32[256,512]{1,0:T(8,128)S(1)} %fusion.6), channel_id=1, source_target_pairs={{0,26},{2,28},{4,30},{6,0},{8,2},{10,4},{12,6},{14,8},{16,10},{18,... | collective-permute-start | bytes 1572872 | tf_op jit(solution)/shard_map/ppermute | solution.py:15
  112.0 0.9 collective-permute-start.7
  112.9 14.0 %collective-permute-done.8 = f32[256,512]{1,0:T(8,128)S(1)} collective-permute-done((f32[256,512]{1,0:T(8,128)S(1)}, f32[256,512]{1,0:T(8,128)S(1)}, u32[]{:S(2)}, u32[]{:S(2)}) %collective-permute-start.8) | collective-permute-done | bytes 524320 | tf_op jit(solution)/shard_map/ppermute | solution.py:15
  126.9 0.4 fusion.17
  127.3 0.4 convolution_add_fusion.1
  127.8 1.7 %collective-permute-start.9 = (f32[256,512]{1,0:T(8,128)S(1)}, f32[256,512]{1,0:T(8,128)S(1)}, u32[]{:S(2)}, u32[]{:S(2)}) collective-permute-start(f32[256,512]{1,0:T(8,128)S(1)} %convolution_add_fusion.1), channel_id=1, source_target_pairs={{0,2},{2,4},{4,6},{6,8},{8,10},{10,12},{12,14},{14,16},{16,18},{18... | collective-permute-start | bytes 1572872 | tf_op jit(solution)/shard_map/ppermute | solution.py:15
  129.5 17.1 %collective-permute-done.7 = f32[256,512]{1,0:T(8,128)S(1)} collective-permute-done((f32[256,512]{1,0:T(8,128)S(1)}, f32[256,512]{1,0:T(8,128)S(1)}, u32[]{:S(2)}, u32[]{:S(2)}) %collective-permute-start.7) | collective-permute-done | bytes 524320 | tf_op jit(solution)/shard_map/ppermute | solution.py:15
  146.5 0.4 fusion.18
  147.0 0.4 convolution_add_fusion
  147.4 0.1 collective-permute-start.10
  147.5 0.4 fusion.16
  147.9 0.4 convolution_add_fusion.3
  148.3 9.5 %collective-permute-done.9 = f32[256,512]{1,0:T(8,128)S(1)} collective-permute-done((f32[256,512]{1,0:T(8,128)S(1)}, f32[256,512]{1,0:T(8,128)S(1)}, u32[]{:S(2)}, u32[]{:S(2)}) %collective-permute-start.9) | collective-permute-done | bytes 524320 | tf_op jit(solution)/shard_map/ppermute | solution.py:15
  157.8 3.9 %collective-permute-done.10 = f32[256,512]{1,0:T(8,128)S(1)} collective-permute-done((f32[256,512]{1,0:T(8,128)S(1)}, f32[256,512]{1,0:T(8,128)S(1)}, u32[]{:S(2)}, u32[]{:S(2)}) %collective-permute-start.10) | collective-permute-done | bytes 524320 | tf_op jit(solution)/shard_map/ppermute | solution.py:15
  161.7 1.3 multiply_add_fusion
  (4 shorter events, 0.0 us)
Async XLA Ops:
  8.4 20.0 %all-to-all-start = ((f32[32,16,256]{2,0,1:T(8,128)}), f32[32,16,256]{2,0,1:T(8,128)S(1)}, u32[]{:S(2)}, u32[]{:S(2)}) async-start(f32[32,16,256]{2,0,1:T(8,128)} %bitcast.52), calls=%async_computation | async-start | bytes 1048576 | tf_op jit(solution)/shard_map/all_to_all | solution.py:42
  15.4 1.4 copy-start.6
  15.4 65.9 %all-reduce.3.cloned.1.call-start = ((), (), s32[]{:S(2)}) async-start(), calls=%async_computation.1 | async-start | bytes 2097152 | tf_op jit(solution)/shard_map/psum | solution.py:50
  17.0 0.7 copy-start.7
  28.4 24.6 %collective-permute-start = (f32[512,256]{1,0:T(8,128)S(1)}, f32[512,256]{1,0:T(8,128)S(1)}, u32[]{:S(2)}, u32[]{:S(2)}) collective-permute-start(f32[512,256]{1,0:T(8,128)S(1)} %bitcast.55), channel_id=1, source_target_pairs={{0,30},{2,0},{4,2},{6,4},{8,6},{10,8},{12,10},{14,12},{16,14},{18,... | collective-permute-start | bytes 1572872 | tf_op jit(solution)/shard_map/ppermute | solution.py:15
  29.0 21.5 %collective-permute-start.4 = (f32[4]{0:T(128)S(1)}, f32[4]{0:T(128)S(1)}, u32[]{:S(2)}, u32[]{:S(2)}) collective-permute-start(f32[4]{0:T(128)S(1)} %select_reduce_fusion), channel_id=1, source_target_pairs={{0,30},{2,0},{4,2},{6,4},{8,6},{10,8},{12,10},{14,12},{16,14},{18,... | collective-permute-start | bytes 56 | tf_op jit(solution)/shard_map/ppermute | solution.py:15
  30.5 24.4 %collective-permute-start.2 = (f32[512,256]{1,0:T(8,128)S(1)}, f32[512,256]{1,0:T(8,128)S(1)}, u32[]{:S(2)}, u32[]{:S(2)}) collective-permute-start(f32[512,256]{1,0:T(8,128)S(1)} %bitcast.56), channel_id=1, source_target_pairs={{0,26},{2,28},{4,30},{6,0},{8,2},{10,4},{12,6},{14,8},{16,10},{18,... | collective-permute-start | bytes 1572872 | tf_op jit(solution)/shard_map/ppermute | solution.py:15
  58.7 1.0 copy-start
  59.7 23.0 %collective-permute-start.3 = (f32[256,512]{1,0:T(8,128)S(1)}, f32[256,512]{1,0:T(8,128)S(1)}, u32[]{:S(2)}, u32[]{:S(2)}) collective-permute-start(f32[256,512]{1,0:T(8,128)S(1)} %copy-done), channel_id=1, source_target_pairs={{0,26},{2,28},{4,30},{6,0},{8,2},{10,4},{12,6},{14,8},{16,10},{18,... | collective-permute-start | bytes 1572872 | tf_op jit(solution)/shard_map/ppermute | solution.py:15
  59.7 25.4 %collective-permute-start.1 = (f32[256,512]{1,0:T(8,128)S(1)}, f32[256,512]{1,0:T(8,128)S(1)}, u32[]{:S(2)}, u32[]{:S(2)}) collective-permute-start(f32[256,512]{1,0:T(8,128)S(1)} %copy-done), channel_id=1, source_target_pairs={{0,30},{2,0},{4,2},{6,4},{8,6},{10,8},{12,10},{14,12},{16,14},{18,... | collective-permute-start | bytes 1572872 | tf_op jit(solution)/shard_map/ppermute | solution.py:15
  81.3 1.4 copy-start.2
  82.7 1.9 %copy-start.3 = (f32[256,256]{1,0:T(8,128)S(1)}, f32[256,256]{1,0:T(8,128)}, u32[]{:S(2)}) copy-start(f32[256,256]{1,0:T(8,128)} %get-tuple-element.7) | copy-start | bytes 786436
  83.1 26.3 %collective-permute-start.5 = (f32[256,512]{1,0:T(8,128)S(1)}, f32[256,512]{1,0:T(8,128)S(1)}, u32[]{:S(2)}, u32[]{:S(2)}) collective-permute-start(f32[256,512]{1,0:T(8,128)S(1)} %convolution_add_fusion.5), channel_id=1, source_target_pairs={{0,2},{2,4},{4,6},{6,8},{8,10},{10,12},{12,14},{14,16},{16,18},{18... | collective-permute-start | bytes 1572872 | tf_op jit(solution)/shard_map/ppermute | solution.py:15
  85.1 1.9 %copy-start.5 = (f32[256,256]{1,0:T(8,128)S(1)}, f32[256,256]{1,0:T(8,128)}, u32[]{:S(2)}) copy-start(f32[256,256]{1,0:T(8,128)} %get-tuple-element.10) | copy-start | bytes 786436
  85.5 23.9 %collective-permute-start.6 = (f32[256,512]{1,0:T(8,128)S(1)}, f32[256,512]{1,0:T(8,128)S(1)}, u32[]{:S(2)}, u32[]{:S(2)}) collective-permute-start(f32[256,512]{1,0:T(8,128)S(1)} %convolution_add_fusion.4), channel_id=1, source_target_pairs={{0,6},{2,8},{4,10},{6,12},{8,14},{10,16},{12,18},{14,20},{16,22},{... | collective-permute-start | bytes 1572872 | tf_op jit(solution)/shard_map/ppermute | solution.py:15
  87.0 1.0 copy-start.1
  87.9 21.5 %copy-start.4 = (f32[256,512]{1,0:T(8,128)S(1)}, f32[256,512]{1,0:T(8,128)}, u32[]{:S(2)}) copy-start(f32[256,512]{1,0:T(8,128)} %param.12) | copy-start | bytes 1572868
  109.9 17.0 %collective-permute-start.8 = (f32[256,512]{1,0:T(8,128)S(1)}, f32[256,512]{1,0:T(8,128)S(1)}, u32[]{:S(2)}, u32[]{:S(2)}) collective-permute-start(f32[256,512]{1,0:T(8,128)S(1)} %fusion.6), channel_id=1, source_target_pairs={{0,26},{2,28},{4,30},{6,0},{8,2},{10,4},{12,6},{14,8},{16,10},{18,... | collective-permute-start | bytes 1572872 | tf_op jit(solution)/shard_map/ppermute | solution.py:15
  112.0 34.6 %collective-permute-start.7 = (f32[256,512]{1,0:T(8,128)S(1)}, f32[256,512]{1,0:T(8,128)S(1)}, u32[]{:S(2)}, u32[]{:S(2)}) collective-permute-start(f32[256,512]{1,0:T(8,128)S(1)} %fusion.6), channel_id=1, source_target_pairs={{0,30},{2,0},{4,2},{6,4},{8,6},{10,8},{12,10},{14,12},{16,14},{18,... | collective-permute-start | bytes 1572872 | tf_op jit(solution)/shard_map/ppermute | solution.py:15
  127.8 30.1 %collective-permute-start.9 = (f32[256,512]{1,0:T(8,128)S(1)}, f32[256,512]{1,0:T(8,128)S(1)}, u32[]{:S(2)}, u32[]{:S(2)}) collective-permute-start(f32[256,512]{1,0:T(8,128)S(1)} %convolution_add_fusion.1), channel_id=1, source_target_pairs={{0,2},{2,4},{4,6},{6,8},{8,10},{10,12},{12,14},{14,16},{16,18},{18... | collective-permute-start | bytes 1572872 | tf_op jit(solution)/shard_map/ppermute | solution.py:15
  147.4 14.3 %collective-permute-start.10 = (f32[256,512]{1,0:T(8,128)S(1)}, f32[256,512]{1,0:T(8,128)S(1)}, u32[]{:S(2)}, u32[]{:S(2)}) collective-permute-start(f32[256,512]{1,0:T(8,128)S(1)} %convolution_add_fusion), channel_id=1, source_target_pairs={{0,6},{2,8},{4,10},{6,12},{8,14},{10,16},{12,18},{14,20},{16,22},{... | collective-permute-start | bytes 1572872 | tf_op jit(solution)/shard_map/ppermute | solution.py:15
Sparse Core Ops, SparseCore 0:
  58.8 22.4 all-reduce.2

commit v2 on v1

--- a/solution.py
+++ b/solution.py
@@ -20,6 +20,12 @@
         a, b, (((ca,), (cb,)), ((), ())), precision=lax.Precision.HIGH,
         preferred_element_type=jnp.float32,
     )
+
+
+def member_sum(tile):
+    if lax.axis_size("mem") == 2:
+        return tile + shifted(tile, "mem", 1)
+    return lax.psum(tile, "mem")
 
 
 def gap_weights(pair_list, pair_count, band_weight, cov_scale):
@@ -47,7 +53,7 @@
     t1 = mm(p0, p1, 0, 0) * w[1]
     t3 = mm(p0, p3, 0, 0) * w[3]
     t2 = mm(p1, p3, 0, 0) * w_next[2]
-    t0, t1, t2, t3 = lax.psum((t0, t1, t2, t3), "mem")
+    t0, t1, t2, t3 = (member_sum(t) for t in (t0, t1, t2, t3))
     for sweep in range(ITERS):
         x1 = shifted(x0, "space", -1)
         x3 = shifted(x0, "space", -3)

time: 172 us -> 160 us (0.930)
  the two profiles are of different devices: /device:TPU:28 before, /device:TPU:4 now
where the time goes in v2:
time: 160 us
  waiting for transfers between devices  86.7 us (54%)
  starting transfers between devices  56.5 us (35%)
  matrix products  11.5 us (7%)
  local copies, waits for them, and re-layouts  3.1 us (2%)
    ppermute x15, waiting for transfers between devices, shifted(): lax.ppermute(array, axis, [(i, (i + by) % count) for i in range(count)])  78.6 us
    ppermute x15, starting transfers between devices, shifted(): lax.ppermute(array, axis, [(i, (i + by) % count) for i in range(count)])  49.1 us
    dot_general x18, matrix products, mm(): lax.dot_general(a, b, (((ca,), (cb,)), ((), ())), precision=lax.Precision...  11.5 us
    all_to_all x1, waiting for transfers between devices, per_device(): lax.all_to_all(perturb, 'space', split_axis=1, concat_axis=0, tiled=True)  8.1 us
    all_to_all x1, starting transfers between devices, per_device(): lax.all_to_all(perturb, 'space', split_axis=1, concat_axis=0, tiled=True)  7.41 us
  transfers between devices with their start and end apart: 16, of which 8 were waited for; matrix products, arithmetic and copies ran while one was open for 7% of the time, Pallas kernels for 0%

profile of v2, /device:TPU:4, one launch (start us, length us, event | category | flops | bytes accessed | tf_op | source)
XLA Modules:
  0.0 160.0 jit_solution(12897809204313483852)
XLA Ops:
  0.0 1.9 %copy.12 = f32[4,16,8,256]{3,2,0,1:T(8,128)} copy(f32[4,16,8,256]{3,2,1,0:T(8,128)} %bitcast.59) | data formatting | bytes 1048576 | tf_op jit(solution)/shard_map/all_to_all | solution.py:48
  1.9 0.0 copy-start
  1.9 7.4 %all-to-all-start = ((f32[32,16,256]{2,0,1:T(8,128)}), f32[32,16,256]{2,0,1:T(8,128)S(1)}, u32[]{:S(2)}, u32[]{:S(2)}) async-start(f32[32,16,256]{2,0,1:T(8,128)} %bitcast.52), calls=%async_computation | async-start | bytes 1048576 | tf_op jit(solution)/shard_map/all_to_all | solution.py:48
  9.3 0.0 copy-done
  9.3 0.0 copy-start.2
  9.3 1.5 collective-permute-start.3
  10.8 3.3 %collective-permute-start.6 = (f32[256,512]{1,0:T(8,128)S(1)}, f32[256,512]{1,0:T(8,128)S(1)}, u32[]{:S(2)}, u32[]{:S(2)}) collective-permute-start(f32[256,512]{1,0:T(8,128)S(1)} %copy-done), channel_id=1, source_target_pairs={{0,26},{2,28},{4,30},{6,0},{8,2},{10,4},{12,6},{14,8},{16,10},{18,... | collective-permute-start | bytes 1572872 | tf_op jit(solution)/shard_map/ppermute | solution.py:15
  15.4 0.0 copy-done.2
  15.4 0.2 fusion.12
  15.6 8.1 %all-to-all-done = f32[32,16,256]{2,0,1:T(8,128)S(1)} async-done(((f32[32,16,256]{2,0,1:T(8,128)}), f32[32,16,256]{2,0,1:T(8,128)S(1)}, u32[]{:S(2)}, u32[]{:S(2)}) %all-to-all-start) | async-done | bytes 524320 | tf_op jit(solution)/shard_map/all_to_all | solution.py:48
  23.7 0.0 copy-start.3
  23.7 24.3 %collective-permute-start.4 = (f32[512,256]{1,0:T(8,128)S(1)}, f32[512,256]{1,0:T(8,128)S(1)}, u32[]{:S(2)}, u32[]{:S(2)}) collective-permute-start(f32[512,256]{1,0:T(8,128)S(1)} %bitcast.55), channel_id=1, source_target_pairs={{0,26},{2,28},{4,30},{6,0},{8,2},{10,4},{12,6},{14,8},{16,10},{18,... | collective-permute-start | bytes 1572872 | tf_op jit(solution)/shard_map/ppermute | solution.py:15
  48.1 0.0 copy-done.3
  48.1 0.2 select_reduce_fusion.1
  48.2 0.1 collective-permute-start.1
  48.3 0.1 select_reduce_fusion
  48.4 1.7 %collective-permute-start.7 = (f32[4]{0:T(128)S(1)}, f32[4]{0:T(128)S(1)}, u32[]{:S(2)}, u32[]{:S(2)}) collective-permute-start(f32[4]{0:T(128)S(1)} %select_reduce_fusion), channel_id=1, source_target_pairs={{0,30},{2,0},{4,2},{6,4},{8,6},{10,8},{12,10},{14,12},{16,14},{18,... | collective-permute-start | bytes 56 | tf_op jit(solution)/shard_map/ppermute | solution.py:15
  50.1 0.6 fusion.14
  50.7 11.1 %collective-permute-done.7 = f32[4]{0:T(128)S(1)} collective-permute-done((f32[4]{0:T(128)S(1)}, f32[4]{0:T(128)S(1)}, u32[]{:S(2)}, u32[]{:S(2)}) %collective-permute-start.7) | collective-permute-done | bytes 48 | tf_op jit(solution)/shard_map/ppermute | solution.py:15
  61.8 0.6 slice.27
  62.3 0.0 collective-permute-done.4
  62.3 1.2 convolution_multiply_fusion.1
  63.6 0.1 collective-permute-start.5
  63.7 0.0 collective-permute-done.1
  63.7 1.2 convolution_multiply_fusion
  64.9 0.6 collective-permute-start.8
  65.5 1.2 fusion.9
  66.7 0.1 collective-permute-start
  66.8 1.2 convolution_multiply_fusion.2
  68.0 0.0 collective-permute-done.5
  68.0 0.6 collective-permute-start.2
  68.6 0.0 collective-permute-done.8
  68.6 0.0 collective-permute-done.3
  68.6 0.4 fusion.18
  69.1 0.4 convolution_add_fusion.3
  69.5 5.7 %collective-permute-start.10 = (f32[256,512]{1,0:T(8,128)S(1)}, f32[256,512]{1,0:T(8,128)S(1)}, u32[]{:S(2)}, u32[]{:S(2)}) collective-permute-start(f32[256,512]{1,0:T(8,128)S(1)} %convolution_add_fusion.3), channel_id=1, source_target_pairs={{0,6},{2,8},{4,10},{6,12},{8,14},{10,16},{12,18},{14,20},{16,22},{... | collective-permute-start | bytes 1572872 | tf_op jit(solution)/shard_map/ppermute | solution.py:15
  75.2 0.0 collective-permute-done.2
  75.2 0.0 collective-permute-done.6
  75.2 0.4 fusion.17
  75.6 0.4 convolution_add_fusion.4
  76.0 3.2 %collective-permute-start.9 = (f32[256,512]{1,0:T(8,128)S(1)}, f32[256,512]{1,0:T(8,128)S(1)}, u32[]{:S(2)}, u32[]{:S(2)}) collective-permute-start(f32[256,512]{1,0:T(8,128)S(1)} %convolution_add_fusion.4), channel_id=1, source_target_pairs={{0,2},{2,4},{4,6},{6,8},{8,10},{10,12},{12,14},{14,16},{16,18},{18... | collective-permute-start | bytes 1572872 | tf_op jit(solution)/shard_map/ppermute | solution.py:15
  79.2 0.0 collective-permute-done
  79.2 0.4 fusion.15
  79.6 0.0 copy-start.1
  79.7 0.4 fusion.16
  80.0 14.8 %collective-permute-done.10 = f32[256,512]{1,0:T(8,128)S(1)} collective-permute-done((f32[256,512]{1,0:T(8,128)S(1)}, f32[256,512]{1,0:T(8,128)S(1)}, u32[]{:S(2)}, u32[]{:S(2)}) %collective-permute-start.10) | collective-permute-done | bytes 524320 | tf_op jit(solution)/shard_map/ppermute | solution.py:15
  94.9 6.9 %collective-permute-done.9 = f32[256,512]{1,0:T(8,128)S(1)} collective-permute-done((f32[256,512]{1,0:T(8,128)S(1)}, f32[256,512]{1,0:T(8,128)S(1)}, u32[]{:S(2)}, u32[]{:S(2)}) %collective-permute-start.9) | collective-permute-done | bytes 524320 | tf_op jit(solution)/shard_map/ppermute | solution.py:15
  101.8 0.0 copy-done.1
  101.8 0.5 fusion.8
  102.3 5.4 %collective-permute-start.12 = (f32[256,512]{1,0:T(8,128)S(1)}, f32[256,512]{1,0:T(8,128)S(1)}, u32[]{:S(2)}, u32[]{:S(2)}) collective-permute-start(f32[256,512]{1,0:T(8,128)S(1)} %fusion.8), channel_id=1, source_target_pairs={{0,26},{2,28},{4,30},{6,0},{8,2},{10,4},{12,6},{14,8},{16,10},{18,... | collective-permute-start | bytes 1572872 | tf_op jit(solution)/shard_map/ppermute | solution.py:15
  107.8 0.5 collective-permute-start.11
  108.3 10.9 %collective-permute-done.12 = f32[256,512]{1,0:T(8,128)S(1)} collective-permute-done((f32[256,512]{1,0:T(8,128)S(1)}, f32[256,512]{1,0:T(8,128)S(1)}, u32[]{:S(2)}, u32[]{:S(2)}) %collective-permute-start.12) | collective-permute-done | bytes 524320 | tf_op jit(solution)/shard_map/ppermute | solution.py:15
  119.2 0.4 fusion.21
  119.6 0.4 convolution_add_fusion.1
  120.0 2.2 %collective-permute-start.13 = (f32[256,512]{1,0:T(8,128)S(1)}, f32[256,512]{1,0:T(8,128)S(1)}, u32[]{:S(2)}, u32[]{:S(2)}) collective-permute-start(f32[256,512]{1,0:T(8,128)S(1)} %convolution_add_fusion.1), channel_id=1, source_target_pairs={{0,2},{2,4},{4,6},{6,8},{8,10},{10,12},{12,14},{14,16},{16,18},{18... | collective-permute-start | bytes 1572872 | tf_op jit(solution)/shard_map/ppermute | solution.py:15
  122.2 20.5 %collective-permute-done.11 = f32[256,512]{1,0:T(8,128)S(1)} collective-permute-done((f32[256,512]{1,0:T(8,128)S(1)}, f32[256,512]{1,0:T(8,128)S(1)}, u32[]{:S(2)}, u32[]{:S(2)}) %collective-permute-start.11) | collective-permute-done | bytes 524320 | tf_op jit(solution)/shard_map/ppermute | solution.py:15
  142.7 0.4 fusion.22
  143.1 0.4 convolution_add_fusion
  143.6 0.1 collective-permute-start.14
  143.6 0.4 fusion.20
  144.0 0.4 fusion.19
  144.4 6.8 %collective-permute-done.13 = f32[256,512]{1,0:T(8,128)S(1)} collective-permute-done((f32[256,512]{1,0:T(8,128)S(1)}, f32[256,512]{1,0:T(8,128)S(1)}, u32[]{:S(2)}, u32[]{:S(2)}) %collective-permute-start.13) | collective-permute-done | bytes 524320 | tf_op jit(solution)/shard_map/ppermute | solution.py:15
  151.2 7.5 %collective-permute-done.14 = f32[256,512]{1,0:T(8,128)S(1)} collective-permute-done((f32[256,512]{1,0:T(8,128)S(1)}, f32[256,512]{1,0:T(8,128)S(1)}, u32[]{:S(2)}, u32[]{:S(2)}) %collective-permute-start.14) | collective-permute-done | bytes 524320 | tf_op jit(solution)/shard_map/ppermute | solution.py:15
  158.7 1.3 multiply_add_fusion
  (5 shorter events, 0.1 us)
Async XLA Ops:
  1.9 7.4 %copy-start = (f32[256,512]{1,0:T(8,128)S(1)}, f32[256,512]{1,0:T(8,128)}, u32[]{:S(2)}) copy-start(f32[256,512]{1,0:T(8,128)} %param.13) | copy-start | bytes 1572868
  1.9 21.8 %all-to-all-start = ((f32[32,16,256]{2,0,1:T(8,128)}), f32[32,16,256]{2,0,1:T(8,128)S(1)}, u32[]{:S(2)}, u32[]{:S(2)}) async-start(f32[32,16,256]{2,0,1:T(8,128)} %bitcast.52), calls=%async_computation | async-start | bytes 1048576 | tf_op jit(solution)/shard_map/all_to_all | solution.py:48
  9.3 6.1 %copy-start.2 = (s32[4,3]{1,0:T(4,128)S(1)}, s32[4,3]{1,0:T(4,128)}, u32[]{:S(2)}) copy-start(s32[4,3]{1,0:T(4,128)} %param.8) | copy-start | bytes 148
  9.3 59.3 %collective-permute-start.3 = (f32[256,512]{1,0:T(8,128)S(1)}, f32[256,512]{1,0:T(8,128)S(1)}, u32[]{:S(2)}, u32[]{:S(2)}) collective-permute-start(f32[256,512]{1,0:T(8,128)S(1)} %copy-done), channel_id=1, source_target_pairs={{0,30},{2,0},{4,2},{6,4},{8,6},{10,8},{12,10},{14,12},{16,14},{18,... | collective-permute-start | bytes 1572872 | tf_op jit(solution)/shard_map/ppermute | solution.py:15
  10.8 64.4 %collective-permute-start.6 = (f32[256,512]{1,0:T(8,128)S(1)}, f32[256,512]{1,0:T(8,128)S(1)}, u32[]{:S(2)}, u32[]{:S(2)}) collective-permute-start(f32[256,512]{1,0:T(8,128)S(1)} %copy-done), channel_id=1, source_target_pairs={{0,26},{2,28},{4,30},{6,0},{8,2},{10,4},{12,6},{14,8},{16,10},{18,... | collective-permute-start | bytes 1572872 | tf_op jit(solution)/shard_map/ppermute | solution.py:15
  23.7 24.3 %copy-start.3 = (f32[8]{0:T(128)S(1)}, f32[8]{0:T(128)}, u32[]{:S(2)}) copy-start(f32[8]{0:T(128)} %param.10) | copy-start | bytes 100
  23.7 38.6 %collective-permute-start.4 = (f32[512,256]{1,0:T(8,128)S(1)}, f32[512,256]{1,0:T(8,128)S(1)}, u32[]{:S(2)}, u32[]{:S(2)}) collective-permute-start(f32[512,256]{1,0:T(8,128)S(1)} %bitcast.55), channel_id=1, source_target_pairs={{0,26},{2,28},{4,30},{6,0},{8,2},{10,4},{12,6},{14,8},{16,10},{18,... | collective-permute-start | bytes 1572872 | tf_op jit(solution)/shard_map/ppermute | solution.py:15
  48.2 15.4 %collective-permute-start.1 = (f32[512,256]{1,0:T(8,128)S(1)}, f32[512,256]{1,0:T(8,128)S(1)}, u32[]{:S(2)}, u32[]{:S(2)}) collective-permute-start(f32[512,256]{1,0:T(8,128)S(1)} %bitcast.56), channel_id=1, source_target_pairs={{0,30},{2,0},{4,2},{6,4},{8,6},{10,8},{12,10},{14,12},{16,14},{18,... | collective-permute-start | bytes 1572872 | tf_op jit(solution)/shard_map/ppermute | solution.py:15
  48.4 13.3 %collective-permute-start.7 = (f32[4]{0:T(128)S(1)}, f32[4]{0:T(128)S(1)}, u32[]{:S(2)}, u32[]{:S(2)}) collective-permute-start(f32[4]{0:T(128)S(1)} %select_reduce_fusion), channel_id=1, source_target_pairs={{0,30},{2,0},{4,2},{6,4},{8,6},{10,8},{12,10},{14,12},{16,14},{18,... | collective-permute-start | bytes 56 | tf_op jit(solution)/shard_map/ppermute | solution.py:15
  63.6 4.4 %collective-permute-start.5 = (f32[256,256]{1,0:T(8,128)S(1)}, f32[256,256]{1,0:T(8,128)S(1)}, u32[]{:S(2)}, u32[]{:S(2)}) collective-permute-start(f32[256,256]{1,0:T(8,128)S(1)} %convolution_multiply_fusion.1), channel_id=1, source_target_pairs={{0,1},{1,0},{2,3},{3,2},{4,5},{5,4},{6,7},{7,6},{8,9},{9,8},{10,11... | collective-permute-start | bytes 786440 | tf_op jit(solution)/shard_map/ppermute | solution.py:15
  64.9 3.6 %collective-permute-start.8 = (f32[256,256]{1,0:T(8,128)S(1)}, f32[256,256]{1,0:T(8,128)S(1)}, u32[]{:S(2)}, u32[]{:S(2)}) collective-permute-start(f32[256,256]{1,0:T(8,128)S(1)} %convolution_multiply_fusion), channel_id=1, source_target_pairs={{0,1},{1,0},{2,3},{3,2},{4,5},{5,4},{6,7},{7,6},{8,9},{9,8},{10,11... | collective-permute-start | bytes 786440 | tf_op jit(solution)/shard_map/ppermute | solution.py:15
  66.7 12.5 %collective-permute-start = (f32[256,256]{1,0:T(8,128)S(1)}, f32[256,256]{1,0:T(8,128)S(1)}, u32[]{:S(2)}, u32[]{:S(2)}) collective-permute-start(f32[256,256]{1,0:T(8,128)S(1)} %fusion.9), channel_id=1, source_target_pairs={{0,1},{1,0},{2,3},{3,2},{4,5},{5,4},{6,7},{7,6},{8,9},{9,8},{10,11... | collective-permute-start | bytes 786440 | tf_op jit(solution)/shard_map/ppermute | solution.py:15
  68.0 7.2 %collective-permute-start.2 = (f32[256,256]{1,0:T(8,128)S(1)}, f32[256,256]{1,0:T(8,128)S(1)}, u32[]{:S(2)}, u32[]{:S(2)}) collective-permute-start(f32[256,256]{1,0:T(8,128)S(1)} %convolution_multiply_fusion.2), channel_id=1, source_target_pairs={{0,1},{1,0},{2,3},{3,2},{4,5},{5,4},{6,7},{7,6},{8,9},{9,8},{10,11... | collective-permute-start | bytes 786440 | tf_op jit(solution)/shard_map/ppermute | solution.py:15
  69.5 25.4 %collective-permute-start.10 = (f32[256,512]{1,0:T(8,128)S(1)}, f32[256,512]{1,0:T(8,128)S(1)}, u32[]{:S(2)}, u32[]{:S(2)}) collective-permute-start(f32[256,512]{1,0:T(8,128)S(1)} %convolution_add_fusion.3), channel_id=1, source_target_pairs={{0,6},{2,8},{4,10},{6,12},{8,14},{10,16},{12,18},{14,20},{16,22},{... | collective-permute-start | bytes 1572872 | tf_op jit(solution)/shard_map/ppermute | solution.py:15
  76.0 25.8 %collective-permute-start.9 = (f32[256,512]{1,0:T(8,128)S(1)}, f32[256,512]{1,0:T(8,128)S(1)}, u32[]{:S(2)}, u32[]{:S(2)}) collective-permute-start(f32[256,512]{1,0:T(8,128)S(1)} %convolution_add_fusion.4), channel_id=1, source_target_pairs={{0,2},{2,4},{4,6},{6,8},{8,10},{10,12},{12,14},{14,16},{16,18},{18... | collective-permute-start | bytes 1572872 | tf_op jit(solution)/shard_map/ppermute | solution.py:15
  79.6 22.2 %copy-start.1 = (f32[256,512]{1,0:T(8,128)S(1)}, f32[256,512]{1,0:T(8,128)}, u32[]{:S(2)}) copy-start(f32[256,512]{1,0:T(8,128)} %param.12) | copy-start | bytes 1572868
  102.3 16.8 %collective-permute-start.12 = (f32[256,512]{1,0:T(8,128)S(1)}, f32[256,512]{1,0:T(8,128)S(1)}, u32[]{:S(2)}, u32[]{:S(2)}) collective-permute-start(f32[256,512]{1,0:T(8,128)S(1)} %fusion.8), channel_id=1, source_target_pairs={{0,26},{2,28},{4,30},{6,0},{8,2},{10,4},{12,6},{14,8},{16,10},{18,... | collective-permute-start | bytes 1572872 | tf_op jit(solution)/shard_map/ppermute | solution.py:15
  107.8 34.9 %collective-permute-start.11 = (f32[256,512]{1,0:T(8,128)S(1)}, f32[256,512]{1,0:T(8,128)S(1)}, u32[]{:S(2)}, u32[]{:S(2)}) collective-permute-start(f32[256,512]{1,0:T(8,128)S(1)} %fusion.8), channel_id=1, source_target_pairs={{0,30},{2,0},{4,2},{6,4},{8,6},{10,8},{12,10},{14,12},{16,14},{18,... | collective-permute-start | bytes 1572872 | tf_op jit(solution)/shard_map/ppermute | solution.py:15
  120.0 31.2 %collective-permute-start.13 = (f32[256,512]{1,0:T(8,128)S(1)}, f32[256,512]{1,0:T(8,128)S(1)}, u32[]{:S(2)}, u32[]{:S(2)}) collective-permute-start(f32[256,512]{1,0:T(8,128)S(1)} %convolution_add_fusion.1), channel_id=1, source_target_pairs={{0,2},{2,4},{4,6},{6,8},{8,10},{10,12},{12,14},{14,16},{16,18},{18... | collective-permute-start | bytes 1572872 | tf_op jit(solution)/shard_map/ppermute | solution.py:15
  143.6 15.2 %collective-permute-start.14 = (f32[256,512]{1,0:T(8,128)S(1)}, f32[256,512]{1,0:T(8,128)S(1)}, u32[]{:S(2)}, u32[]{:S(2)}) collective-permute-start(f32[256,512]{1,0:T(8,128)S(1)} %convolution_add_fusion), channel_id=1, source_target_pairs={{0,6},{2,8},{4,10},{6,12},{8,14},{10,16},{12,18},{14,20},{16,22},{... | collective-permute-start | bytes 1572872 | tf_op jit(solution)/shard_map/ppermute | solution.py:15

commit v3 on v2

--- a/solution.py
+++ b/solution.py
@@ -1,6 +1,9 @@
+import functools
 import jax
 import jax.numpy as jnp
 from jax import lax
+from jax.experimental import pallas as pl
+from jax.experimental.pallas import tpu as pltpu
 from jax.sharding import PartitionSpec as P
 
 BLOCK = 256
@@ -42,7 +45,7 @@
     return jnp.sum(jnp.where(gap[:, None] == gaps[None, :], slot_weight[:, None], 0.0), axis=0)
 
 
-def per_device(perturb, pair_list, pair_count, band_weight, cov_scale, target, first_guess):
+def by_collectives(perturb, pair_list, pair_count, band_weight, cov_scale, target, first_guess):
     w = gap_weights(pair_list, pair_count, band_weight, cov_scale)
     w_next = shifted(w, "space", -1)
     p0 = lax.all_to_all(perturb, "space", split_axis=1, concat_axis=0, tiled=True)
@@ -63,6 +66,300 @@
         x0 = x0 + 0.5 * (target - x0 - (own + back1 + back3))
     return x0
 
+GROUP = REACH_DEV + 1
+NEAR = 2 * REACH_DEV + 1
+SPANS = ((0, 0), (1, 1), (3, 2))
+
+
+class Mover:
+    def __init__(self, send_sem, recv_sem, local_sem):
+        self.send_sem, self.recv_sem, self.local_sem = send_sem, recv_sem, local_sem
+        self.sent = 0
+        self.local = 0
+        self.open = []
+
+    def to(self, source, target, device):
+        copy = pltpu.make_async_remote_copy(
+            src_ref=source, dst_ref=target,
+            send_sem=self.send_sem.at[self.sent], recv_sem=self.recv_sem.at[self.sent],
+            device_id=device, device_id_type=pl.DeviceIdType.MESH,
+        )
+        self.sent += 1
+        copy.start()
+        self.open.append(copy)
+        return copy
+
+    def here(self, source, target):
+        copy = pltpu.make_async_copy(source, target, self.local_sem.at[self.local])
+        self.local += 1
+        copy.start()
+        return copy
+
+
+def split(value):
+    high = value.astype(jnp.bfloat16)
+    return high, (value - high.astype(jnp.float32)).astype(jnp.bfloat16)
+
+
+def dot(a, b, ca, cb):
+    return lax.dot_general(a, b, (((ca,), (cb,)), ((), ())), preferred_element_type=jnp.float32)
+
+
+def kernel(planes, perturb, table, guess, target, out, pz, pg, part, part_in, table_next, tiles,
+           tile_hi, tile_lo, xb, tb, halo, xs, acc, px, ret_in, halo_in, final, send_sem, recv_sem,
+           local_sem):
+    space = lax.axis_index("space")
+    mem = lax.axis_index("mem")
+    count = planes * GROUP
+    k = space // GROUP
+    j = space % GROUP
+    rows = perturb.shape[0]
+    width = GROUP * BLOCK
+    cols = xb.shape[2]
+    half = BLOCK // 2
+
+    def plane(r):
+        return (((k + r) % planes) * GROUP + j, mem)
+
+    def chip(q):
+        return (k * GROUP + (j + q) % GROUP, mem)
+
+    partner = (space, 1 - mem)
+    before = ((space + count - 1) % count, mem)
+    after = ((space + 1) % count, mem)
+    barrier = pltpu.get_barrier_semaphore()
+    greeted = [plane(r) for r in range(1, planes)] + [chip(q) for q in range(1, GROUP)]
+    greeted += [partner, before, after]
+    for device in greeted:
+        pl.semaphore_signal(barrier, inc=1, device_id=device, device_id_type=pl.DeviceIdType.MESH)
+    pl.semaphore_wait(barrier, len(greeted))
+
+    move = Mover(send_sem, recv_sem, local_sem)
+
+    def at(block, size):
+        return pl.ds(pl.multiple_of(block * BLOCK, BLOCK), size * BLOCK)
+
+    from_plane = {}
+    for r in range(planes - 1, 0, -1):
+        there = (k + planes - r) % planes
+        nxt = (there + 1) % planes
+        device = plane(planes - r)
+        from_plane[r] = (
+            move.to(perturb.at[:, at(there * GROUP, GROUP)], pz.at[r, :, pl.ds(0, width)], device),
+            move.to(perturb.at[:, at(nxt * GROUP, REACH_DEV)],
+                    pz.at[r, :, pl.ds(width, REACH_DEV * BLOCK)], device),
+        )
+    table_copy = move.to(table, table_next, before)
+    own = (
+        move.here(perturb.at[:, at(k * GROUP, GROUP)], pz.at[0, :, pl.ds(0, width)]),
+        move.here(perturb.at[:, at(((k + 1) % planes) * GROUP, REACH_DEV)],
+                  pz.at[0, :, pl.ds(width, REACH_DEV * BLOCK)]),
+    )
+    for copy in own:
+        copy.wait()
+
+    def spread(r):
+        copies = []
+        for q in range(1, GROUP):
+            there = (j + q) % GROUP
+            copies.append(move.to(pz.at[r, :, at(there, 2)],
+                                  pg.at[r, q, :, pl.ds(0, 2 * BLOCK)], chip(q)))
+            copies.append(move.to(pz.at[r, :, at(there + REACH_DEV, 1)],
+                                  pg.at[r, q, :, pl.ds(2 * BLOCK, BLOCK)], chip(q)))
+        mine = (move.here(pz.at[r, :, at(j, 2)], pg.at[r, 0, :, pl.ds(0, 2 * BLOCK)]),
+                move.here(pz.at[r, :, at(j + REACH_DEV, 1)],
+                          pg.at[r, 0, :, pl.ds(2 * BLOCK, BLOCK)]))
+        return copies, mine
+
+    def products(r, copies):
+        for copy in copies[0]:
+            copy.wait_recv()
+        for copy in copies[1]:
+            copy.wait()
+        value = pg[r].reshape(GROUP * rows, 3 * BLOCK)
+        high, low = split(value)
+        left = jnp.concatenate([high[:, : 2 * BLOCK], high[:, : 2 * BLOCK], low[:, : 2 * BLOCK]], 0)
+        right = jnp.concatenate([high, low, high], 0)
+        wide = dot(left[:, :BLOCK], right, 0, 0)
+        last = dot(left[:, BLOCK:], right[:, 2 * BLOCK :], 0, 0)
+        if r == 0:
+            part[:, : 3 * BLOCK] = wide
+            part[:, 3 * BLOCK :] = last
+        else:
+            part[:, : 3 * BLOCK] += wide
+            part[:, 3 * BLOCK :] += last
+
+    spreading = {0: spread(0)}
+
+    def share(source, blocks):
+        copies = []
+        for q in range(1, GROUP):
+            there = (j + q) % GROUP
+            piece = source.at[:, pl.ds(pl.multiple_of(there * cols, cols), cols)]
+            copies.append(move.to(piece, blocks.at[j], chip(q)))
+        mine = move.here(source.at[:, pl.ds(pl.multiple_of(j * cols, cols), cols)], blocks.at[j])
+        return copies, mine
+
+    guesses = share(guess, xb)
+    targets = share(target, tb)
+    order = list(range(1, planes))
+    for r in order:
+        for copy in from_plane[r]:
+            copy.wait_recv()
+        spreading[r] = spread(r)
+        products(r - 1, spreading[r - 1])
+    for copy in guesses[0]:
+        copy.wait_recv()
+    guesses[1].wait()
+    halo_copy = move.to(xb.at[pl.ds(0, REACH_DEV)], halo, plane(planes - 1))
+    for n in range(GROUP):
+        xs[n, :, :cols], xs[n, :, cols:] = split(xb[n])
+    products(planes - 1, spreading[planes - 1])
+
+    mine = pl.ds(pl.multiple_of(mem * half, half), half)
+    other = pl.ds(pl.multiple_of((1 - mem) * half, half), half)
+    part_copy = move.to(part.at[other], part_in, partner)
+    table_copy.wait_recv()
+    part_copy.wait_recv()
+    rates = (table[0:1], table[1:2], table[3:4], table_next[2:3])
+    for n, rate in enumerate(rates):
+        span = pl.ds(n * BLOCK, BLOCK)
+        tiles[j, mine, span] = (part[mine, span] + part_in[:, span]) * rate
+    gather = {q: move.to(tiles.at[j, mine], tiles.at[j, mine], chip(q)) for q in range(1, GROUP)}
+    pair = {0: move.to(tiles.at[j, mine], tiles.at[j, mine], partner)}
+
+    halo_copy.wait_recv()
+    for n in range(REACH_DEV):
+        xs[GROUP + n, :, :cols], xs[GROUP + n, :, cols:] = split(halo[n])
+    for n in range(NEAR):
+        acc[0, n] = jnp.zeros_like(acc[0, n])
+        acc[1, n] = jnp.zeros_like(acc[1, n])
+
+    def times(high, low, x, side):
+        both = dot(high, x, side, 0)
+        return both[:, :cols] + both[:, cols:] + dot(low, x[:, :cols], side, 0)
+
+    def apply(sweep, i):
+        xa, xb_, xc = xs[i], xs[i + 1], xs[i + 3]
+        high, low = tile_hi[i], tile_lo[i]
+        B = BLOCK
+        acc[sweep, i] += (times(high[:, :B], low[:, :B], xa, 1)
+                          + times(high[:, B : 2 * B], low[:, B : 2 * B], xb_, 1)
+                          + times(high[:, 2 * B : 3 * B], low[:, 2 * B : 3 * B], xc, 1))
+        down = times(high[:, B : 3 * B], low[:, B : 3 * B], xa, 0)
+        acc[sweep, i + 1] += down[:B] + times(high[:, 3 * B :], low[:, 3 * B :], xc, 1)
+        acc[sweep, i + 3] += down[B:] + times(high[:, 3 * B :], low[:, 3 * B :], xb_, 0)
+
+    for q in range(GROUP):
+        i = (j + GROUP - q) % GROUP
+        if q + 1 < GROUP:
+            gather[q + 1].wait_recv()
+            there = (j + GROUP - q - 1) % GROUP
+            pair[q + 1] = move.to(tiles.at[there, mine], tiles.at[there, mine], partner)
+        pair[q].wait_recv()
+        tile_hi[i], tile_lo[i] = split(tiles[i])
+        apply(0, i)
+
+    for copy in targets[0]:
+        copy.wait_recv()
+    targets[1].wait()
+    back = move.to(acc.at[0, pl.ds(GROUP, REACH_DEV)], ret_in.at[0], plane(1))
+    for n in range(GROUP):
+        px[n] = xb[n] + 0.5 * (tb[n] - xb[n] - acc[0, n])
+    ahead = move.to(px.at[pl.ds(0, REACH_DEV)], halo_in, plane(planes - 1))
+    final[GROUP - 1] = px[GROUP - 1]
+    xs[GROUP - 1, :, :cols], xs[GROUP - 1, :, cols:] = split(px[GROUP - 1])
+    back.wait_recv()
+    for n in range(REACH_DEV):
+        now = px[n] - 0.5 * ret_in[0, n]
+        final[n] = now
+        xs[n, :, :cols], xs[n, :, cols:] = split(now)
+    ahead.wait_recv()
+    for n in range(REACH_DEV):
+        now = halo_in[n] - 0.5 * acc[0, GROUP + n]
+        xs[GROUP + n, :, :cols], xs[GROUP + n, :, cols:] = split(now)
+
+    @pl.loop(0, GROUP)
+    def _(step):
+        apply(1, step)
+
+    back = move.to(acc.at[1, pl.ds(GROUP, REACH_DEV)], ret_in.at[1], plane(1))
+    for n in range(GROUP):
+        now = final[n]
+        final[n] = now + 0.5 * (tb[n] - now - acc[1, n])
+    back.wait_recv()
+    for n in range(REACH_DEV):
+        final[n] = final[n] - 0.5 * ret_in[1, n]
+    place = pl.ds(pl.multiple_of(j * cols, cols), cols)
+    done = []
+    for q in range(1, GROUP):
+        there = (j + q) % GROUP
+        done.append(move.to(final.at[there], out.at[:, place], chip(q)))
+    last = move.here(final.at[j], out.at[:, place])
+    for copy in done:
+        copy.wait_recv()
+    last.wait()
+    for copy in move.open:
+        copy.wait_send()
+
+
+def in_one_kernel(perturb, pair_list, pair_count, band_weight, cov_scale, target, first_guess):
+    w = gap_weights(pair_list, pair_count, band_weight, cov_scale)
+    table = jnp.broadcast_to(jnp.pad(w, (0, 8 - w.shape[0]))[:, None], (8, BLOCK))
+    planes = lax.axis_size("space") // GROUP
+    rows = perturb.shape[0]
+    cols = first_guess.shape[1] // GROUP
+    f32, bf16 = jnp.float32, jnp.bfloat16
+    sends = 2 * (planes - 1) + 1 + planes * 2 * (GROUP - 1) + 2 * (GROUP - 1) + 1 + 1
+    sends += 2 * (GROUP - 1) + 1 + 3 + GROUP - 1
+    locals_ = 2 + 2 * planes + 2 + 1
+    vmem = pl.BlockSpec(memory_space=pltpu.VMEM)
+    return pl.pallas_call(
+        functools.partial(kernel, planes),
+        out_shape=jax.ShapeDtypeStruct(first_guess.shape, f32),
+        in_specs=[vmem] * 4,
+        out_specs=vmem,
+        scratch_shapes=[
+            pltpu.VMEM((planes, rows, NEAR * BLOCK), f32),
+            pltpu.VMEM((planes, GROUP, rows, 3 * BLOCK), f32),
+            pltpu.VMEM((BLOCK, 4 * BLOCK), f32),
+            pltpu.VMEM((BLOCK // 2, 4 * BLOCK), f32),
+            pltpu.VMEM((8, BLOCK), f32),
+            pltpu.VMEM((GROUP, BLOCK, 4 * BLOCK), f32),
+            pltpu.VMEM((GROUP, BLOCK, 4 * BLOCK), bf16),
+            pltpu.VMEM((GROUP, BLOCK, 4 * BLOCK), bf16),
+            pltpu.VMEM((GROUP, BLOCK, cols), f32),
+            pltpu.VMEM((GROUP, BLOCK, cols), f32),
+            pltpu.VMEM((REACH_DEV, BLOCK, cols), f32),
+            pltpu.VMEM((NEAR, BLOCK, 2 * cols), bf16),
+            pltpu.VMEM((2, NEAR, BLOCK, cols), f32),
+            pltpu.VMEM((GROUP, BLOCK, cols), f32),
+            pltpu.VMEM((2, REACH_DEV, BLOCK, cols), f32),
+            pltpu.VMEM((REACH_DEV, BLOCK, cols), f32),
+            pltpu.VMEM((GROUP, BLOCK, cols), f32),
+            pltpu.SemaphoreType.DMA((sends,)),
+            pltpu.SemaphoreType.DMA((sends,)),
+            pltpu.SemaphoreType.DMA((locals_,)),
+        ],
+        compiler_params=pltpu.CompilerParams(
+            collective_id=0, has_side_effects=True, vmem_limit_bytes=48 * 1024 * 1024
+        ),
+    )(perturb, table, first_guess, target)
+
+
+def fits(perturb, field):
+    planes, rest = divmod(lax.axis_size("space"), GROUP)
+    return (
+        lax.axis_size("mem") == 2 and rest == 0 and planes >= 2
+        and perturb.shape[0] % 8 == 0 and field.shape[1] % (GROUP * 128) == 0
+        and field.shape[0] == BLOCK
+    )
+
+
+def per_device(perturb, pair_list, pair_count, band_weight, cov_scale, target, first_guess):
+    whole = in_one_kernel if fits(perturb, first_guess) else by_collectives
+    return whole(perturb, pair_list, pair_count, band_weight, cov_scale, target, first_guess)
+
 
 def solution(mesh):
     in_specs = (

time: 160 us -> 112 us (0.70)
  the two profiles are of different devices: /device:TPU:4 before, /device:TPU:28 now
where the time goes in v3:
time: 112 us; the launch traced here: 111 us
  Pallas kernels  104 us (93%)
  local copies, waits for them, and re-layouts  4.67 us (4%)
  between operations  1.34 us (1%)
    pallas_call x1, Pallas kernels, in_one_kernel(): pl.pallas_call(functools.partial(kernel, planes), out_shape=jax.ShapeDtyp...  104 us
    unnamed x11, local copies, waits for them, and re-layouts  4.59 us

profile of v3, /device:TPU:28, one launch (start us, length us, event | category | flops | bytes accessed | tf_op | source)
XLA Modules:
  0.0 110.6 jit_solution(6042087477468832945)
XLA Ops:
  0.7 0.0 copy-start.3
  1.3 0.0 copy-done.3
  1.3 0.2 fusion.1
  1.6 0.0 copy-start.4
  1.6 0.7 copy-done.4
  2.2 0.2 select_reduce_fusion.1
  2.4 0.1 select_reduce_fusion
  2.5 0.1 broadcast_in_dim.39.table
  2.6 0.0 copy-start
  2.6 1.0 copy-done
  3.6 0.0 copy-start.1
  3.6 1.0 copy-done.1
  4.7 0.0 copy-start.2
  4.7 1.0 copy-done.2
  5.7 104.1 %shard_map.73 = f32[256,512]{1,0:T(8,128)S(1)} custom-call(f32[32,4096]{1,0:T(8,128)S(1)} %copy-done, f32[8,256]{1,0:T(8,128)S(1)} %broadcast_in_dim.39.table, f32[256,512]{1,0:T(8,128)S(1)} %copy-done.1, f32[256,512]{1,0:T(8,128)S(1)} %copy-done.2), custom_call_target="tpu_custom_call" | custom-call | tf_op jit(solution)/shard_map/pallas_call | solution.py:317
  109.8 0.8 copy.11
  (2 shorter events, 0.0 us)
Async XLA Ops:
  0.7 0.7 copy-start.3
  1.6 0.7 copy-start.4
  2.6 1.0 copy-start
  3.6 1.0 copy-start.1
  4.7 1.0 copy-start.2

commit v4 on v3

--- a/solution.py
+++ b/solution.py
@@ -225,8 +225,15 @@
     for n, rate in enumerate(rates):
         span = pl.ds(n * BLOCK, BLOCK)
         tiles[j, mine, span] = (part[mine, span] + part_in[:, span]) * rate
-    gather = {q: move.to(tiles.at[j, mine], tiles.at[j, mine], chip(q)) for q in range(1, GROUP)}
-    pair = {0: move.to(tiles.at[j, mine], tiles.at[j, mine], partner)}
+    side = j + 1 - 2 * (j % 2)
+    over = (j + 2) % GROUP
+    far = (side + 2) % GROUP
+
+    def tile_to(i, device):
+        return move.to(tiles.at[i, mine], tiles.at[i, mine], device)
+
+    near_copies = [tile_to(j, (k * GROUP + there, mem)) for there in (side, over)]
+    pair = {0: tile_to(j, partner)}
 
     halo_copy.wait_recv()
     for n in range(REACH_DEV):
@@ -250,55 +257,103 @@
         acc[sweep, i + 1] += down[:B] + times(high[:, 3 * B :], low[:, 3 * B :], xc, 1)
         acc[sweep, i + 3] += down[B:] + times(high[:, 3 * B :], low[:, 3 * B :], xb_, 0)
 
-    for q in range(GROUP):
-        i = (j + GROUP - q) % GROUP
-        if q + 1 < GROUP:
-            gather[q + 1].wait_recv()
-            there = (j + GROUP - q - 1) % GROUP
-            pair[q + 1] = move.to(tiles.at[there, mine], tiles.at[there, mine], partner)
-        pair[q].wait_recv()
+    def take(step, i):
+        pair[step].wait_recv()
         tile_hi[i], tile_lo[i] = split(tiles[i])
         apply(0, i)
+
+    take(0, j)
+    for copy in near_copies:
+        copy.wait_recv()
+    onward = tile_to(side + mem * (over - side), (k * GROUP + over + mem * (side - over), mem))
+    pair[1] = tile_to(side, partner)
+    pair[2] = tile_to(over, partner)
+    take(1, side)
+    take(2, over)
+    onward.wait_recv()
+    pair[3] = tile_to(far, partner)
+    take(3, far)
 
     for copy in targets[0]:
         copy.wait_recv()
     targets[1].wait()
-    back = move.to(acc.at[0, pl.ds(GROUP, REACH_DEV)], ret_in.at[0], plane(1))
+    def back(sweep, n):
+        return move.to(acc.at[sweep, GROUP + n], ret_in.at[sweep, n], plane(1))
+
+    backs = [back(0, n) for n in range(2)]
+    aheads = []
     for n in range(GROUP):
         px[n] = xb[n] + 0.5 * (tb[n] - xb[n] - acc[0, n])
-    ahead = move.to(px.at[pl.ds(0, REACH_DEV)], halo_in, plane(planes - 1))
-    final[GROUP - 1] = px[GROUP - 1]
-    xs[GROUP - 1, :, :cols], xs[GROUP - 1, :, cols:] = split(px[GROUP - 1])
-    back.wait_recv()
-    for n in range(REACH_DEV):
-        now = px[n] - 0.5 * ret_in[0, n]
-        final[n] = now
+        if n < REACH_DEV:
+            aheads.append(move.to(px.at[n], halo_in.at[n], plane(planes - 1)))
+    backs.append(back(0, 2))
+
+    def settle(n, now):
         xs[n, :, :cols], xs[n, :, cols:] = split(now)
-    ahead.wait_recv()
-    for n in range(REACH_DEV):
-        now = halo_in[n] - 0.5 * acc[0, GROUP + n]
-        xs[GROUP + n, :, :cols], xs[GROUP + n, :, cols:] = split(now)
-
-    @pl.loop(0, GROUP)
-    def _(step):
-        apply(1, step)
-
-    back = move.to(acc.at[1, pl.ds(GROUP, REACH_DEV)], ret_in.at[1], plane(1))
+        if n < GROUP:
+            final[n] = now + 0.5 * (tb[n] - now)
+
+    def settle_own(n):
+        backs[n].wait_recv()
+        settle(n, px[n] - 0.5 * ret_in[0, n])
+
+    def settle_halo(n):
+        aheads[n].wait_recv()
+        settle(GROUP + n, halo_in[n] - 0.5 * acc[0, GROUP + n])
+
+    place = pl.ds(pl.multiple_of(j * cols, cols), cols)
+    base = move.sent
+    here_sem = local_sem.at[move.local]
+
+    def leave(n, source):
+        return pltpu.make_async_remote_copy(
+            src_ref=final.at[n], dst_ref=out.at[:, place],
+            send_sem=send_sem.at[base + n], recv_sem=recv_sem.at[base + source],
+            device_id=(k * GROUP + n, mem), device_id_type=pl.DeviceIdType.MESH,
+        )
+
+    def stay(n):
+        return pltpu.make_async_copy(final.at[n], out.at[:, place], here_sem)
+
+    def put(n):
+        @pl.when(j != n)
+        def _():
+            leave(n, j).start()
+
+        @pl.when(j == n)
+        def _():
+            stay(n).start()
+
+    move.sent = base + GROUP
+    settle(GROUP - 1, px[GROUP - 1])
+    settle_own(0)
+    settle_own(1)
+    apply(1, 0)
+    settle_own(2)
+    settle_halo(0)
+    apply(1, 1)
+    settle_halo(1)
+    apply(1, 2)
+    backs = {1: back(1, 1)}
+    settle_halo(2)
+    apply(1, 3)
+    backs[0] = back(1, 0)
+    backs[2] = back(1, 2)
+    final[3] = final[3] - 0.5 * acc[1, 3]
+    put(3)
+    for n in (1, 0, 2):
+        backs[n].wait_recv()
+        final[n] = final[n] - 0.5 * (acc[1, n] + ret_in[1, n])
+        put(n)
     for n in range(GROUP):
-        now = final[n]
-        final[n] = now + 0.5 * (tb[n] - now - acc[1, n])
-    back.wait_recv()
-    for n in range(REACH_DEV):
-        final[n] = final[n] - 0.5 * ret_in[1, n]
-    place = pl.ds(pl.multiple_of(j * cols, cols), cols)
-    done = []
-    for q in range(1, GROUP):
-        there = (j + q) % GROUP
-        done.append(move.to(final.at[there], out.at[:, place], chip(q)))
-    last = move.here(final.at[j], out.at[:, place])
-    for copy in done:
-        copy.wait_recv()
-    last.wait()
+        @pl.when(j != n)
+        def _():
+            leave(n, n).wait_send()
+            leave(n, n).wait_recv()
+
+        @pl.when(j == n)
+        def _():
+            stay(n).wait()
     for copy in move.open:
         copy.wait_send()
 
@@ -311,7 +366,7 @@
     cols = first_guess.shape[1] // GROUP
     f32, bf16 = jnp.float32, jnp.bfloat16
     sends = 2 * (planes - 1) + 1 + planes * 2 * (GROUP - 1) + 2 * (GROUP - 1) + 1 + 1
-    sends += 2 * (GROUP - 1) + 1 + 3 + GROUP - 1
+    sends += 3 + GROUP + 1 + 3 * REACH_DEV + GROUP
     locals_ = 2 + 2 * planes + 2 + 1
     vmem = pl.BlockSpec(memory_space=pltpu.VMEM)
     return pl.pallas_call(

time: 112 us -> 105 us (0.938); the launches traced: 111 us -> 105 us
  Pallas kernels: 104 us -> 98.6 us
    pallas_call x1, Pallas kernels: 104 us -> 98.6 us  [in_one_kernel(): pl.pallas_call(functools.partial(kernel, planes), out_shape=jax.ShapeDtyp...]
where the time goes in v4:
time: 105 us
  Pallas kernels  98.6 us (94%)
  local copies, waits for them, and re-layouts  4.67 us (4%)
  between operations  1.34 us (1%)
    pallas_call x1, Pallas kernels, in_one_kernel(): pl.pallas_call(functools.partial(kernel, planes), out_shape=jax.ShapeDtyp...  98.6 us
    unnamed x11, local copies, waits for them, and re-layouts  4.59 us

profile of v4, /device:TPU:28, one launch (start us, length us, event | category | flops | bytes accessed | tf_op | source)
XLA Modules:
  0.0 105.1 jit_solution(12509003940542910515)
XLA Ops:
  0.7 0.0 copy-start.3
  1.3 0.0 copy-done.3
  1.3 0.2 fusion.1
  1.6 0.0 copy-start.4
  1.6 0.7 copy-done.4
  2.2 0.2 select_reduce_fusion.1
  2.4 0.1 select_reduce_fusion
  2.5 0.1 broadcast_in_dim.39.table
  2.6 0.0 copy-start
  2.6 1.0 copy-done
  3.6 0.0 copy-start.1
  3.6 1.0 copy-done.1
  4.7 0.0 copy-start.2
  4.7 1.0 copy-done.2
  5.7 98.6 %shard_map.73 = f32[256,512]{1,0:T(8,128)S(1)} custom-call(f32[32,4096]{1,0:T(8,128)S(1)} %copy-done, f32[8,256]{1,0:T(8,128)S(1)} %broadcast_in_dim.39.table, f32[256,512]{1,0:T(8,128)S(1)} %copy-done.1, f32[256,512]{1,0:T(8,128)S(1)} %copy-done.2), custom_call_target="tpu_custom_call" | custom-call | tf_op jit(solution)/shard_map/pallas_call | solution.py:372
  104.3 0.8 copy.11
  (2 shorter events, 0.0 us)
Async XLA Ops:
  0.7 0.7 copy-start.3
  1.6 0.7 copy-start.4
  2.6 1.0 copy-start
  3.6 1.0 copy-start.1
  4.7 1.0 copy-start.2

commit v5 on v4

--- a/solution.py
+++ b/solution.py
@@ -171,11 +171,13 @@
                           pg.at[r, 0, :, pl.ds(2 * BLOCK, BLOCK)]))
         return copies, mine
 
-    def products(r, copies):
+    def arrive(copies):
         for copy in copies[0]:
             copy.wait_recv()
         for copy in copies[1]:
             copy.wait()
+
+    def products(r):
         value = pg[r].reshape(GROUP * rows, 3 * BLOCK)
         high, low = split(value)
         left = jnp.concatenate([high[:, : 2 * BLOCK], high[:, : 2 * BLOCK], low[:, : 2 * BLOCK]], 0)
@@ -201,20 +203,22 @@
         return copies, mine
 
     guesses = share(guess, xb)
-    targets = share(target, tb)
     order = list(range(1, planes))
     for r in order:
         for copy in from_plane[r]:
             copy.wait_recv()
         spreading[r] = spread(r)
-        products(r - 1, spreading[r - 1])
+        arrive(spreading[r - 1])
+        products(r - 1)
     for copy in guesses[0]:
         copy.wait_recv()
     guesses[1].wait()
     halo_copy = move.to(xb.at[pl.ds(0, REACH_DEV)], halo, plane(planes - 1))
     for n in range(GROUP):
         xs[n, :, :cols], xs[n, :, cols:] = split(xb[n])
-    products(planes - 1, spreading[planes - 1])
+    arrive(spreading[planes - 1])
+    targets = share(target, tb)
+    products(planes - 1)
 
     mine = pl.ds(pl.multiple_of(mem * half, half), half)
     other = pl.ds(pl.multiple_of((1 - mem) * half, half), half)
@@ -369,10 +373,11 @@
     sends += 3 + GROUP + 1 + 3 * REACH_DEV + GROUP
     locals_ = 2 + 2 * planes + 2 + 1
     vmem = pl.BlockSpec(memory_space=pltpu.VMEM)
+    hbm = pl.BlockSpec(memory_space=pltpu.HBM)
     return pl.pallas_call(
         functools.partial(kernel, planes),
         out_shape=jax.ShapeDtypeStruct(first_guess.shape, f32),
-        in_specs=[vmem] * 4,
+        in_specs=[hbm, vmem, hbm, hbm],
         out_specs=vmem,
         scratch_shapes=[
             pltpu.VMEM((planes, rows, NEAR * BLOCK), f32),

time: 105 us -> 109 us (1.038)
  Pallas kernels: 98.6 us -> 102 us
    pallas_call x1, Pallas kernels: 98.6 us -> 102 us  [in_one_kernel(): pl.pallas_call(functools.partial(kernel, planes), out_shape=jax.ShapeDtyp...]
where the time goes in v5:
time: 109 us
  Pallas kernels  102 us (94%)
  local copies, waits for them, and re-layouts  4.67 us (4%)
  between operations  1.34 us (1%)
    pallas_call x1, Pallas kernels, in_one_kernel(): pl.pallas_call(functools.partial(kernel, planes), out_shape=jax.ShapeDtyp...  102 us
    unnamed x11, local copies, waits for them, and re-layouts  4.59 us

profile of v5, /device:TPU:28, one launch (start us, length us, event | category | flops | bytes accessed | tf_op | source)
XLA Modules:
  0.0 108.7 jit_solution(16702432195475197664)
XLA Ops:
  0.7 0.0 copy-start.3
  1.3 0.0 copy-done.3
  1.3 0.2 fusion.1
  1.6 0.0 copy-start.4
  1.6 0.7 copy-done.4
  2.2 0.2 select_reduce_fusion.1
  2.4 0.1 select_reduce_fusion
  2.5 0.1 broadcast_in_dim.39.table
  2.6 0.0 copy-start
  2.6 1.0 copy-done
  3.6 0.0 copy-start.1
  3.6 1.0 copy-done.1
  4.7 0.0 copy-start.2
  4.7 1.0 copy-done.2
  5.7 102.2 %shard_map.73 = f32[256,512]{1,0:T(8,128)S(1)} custom-call(f32[32,4096]{1,0:T(8,128)S(1)} %copy-done, f32[8,256]{1,0:T(8,128)S(1)} %broadcast_in_dim.39.table, f32[256,512]{1,0:T(8,128)S(1)} %copy-done.1, f32[256,512]{1,0:T(8,128)S(1)} %copy-done.2), custom_call_target="tpu_custom_call" | custom-call | tf_op jit(solution)/shard_map/pallas_call | solution.py:377
  107.9 0.8 copy.11
  (2 shorter events, 0.0 us)
Async XLA Ops:
  0.7 0.7 copy-start.3
  1.6 0.7 copy-start.4
  2.6 1.0 copy-start
  3.6 1.0 copy-start.1
  4.7 1.0 copy-start.2
